TPU v7x, 512 devices: a whole 4x4x16 slice. The times are simulated.
512 devices in a mesh: grp: 4 (over x), dev: 128 (over z, y, core).
Axes of the slice: x: 4, y: 4, z: 16, core: 2. Of those that a mesh axis runs over, the one named last changes fastest.
Arguments:
- leaf_emit: float32 [3, 65536], P(None, 'dev'), may hold values from 0 to 1
- leaf_albedo: float32 [3, 65536], P(None, 'dev'), may hold values from 0.2 to 0.9
- leaf_radiosity: float32 [3, 65536], P(None, 'dev'), may hold values from 0.05 to 4
- leaf_area: float32 [65536], P('dev'), may hold values from 0.002 to 0.03
- parent_index: int32 [65536], P('dev'), may hold values from 0 to 255, as said below
- node_position: float32 [3, 98304], P(None, 'dev'), may hold values from -1 to 1
- node_angles: float32 [2, 98304], P(None, 'dev'), may hold values from -3.140625 to 3.140625
- block_receiver: int32 [4, 16384], P('grp', 'dev'), may hold values from 0 to 5
- block_source: int32 [4, 16384], P('grp', 'dev'), may hold values from 0 to 255
- block_count: int32 [4, 128], P('grp', 'dev'), may hold values from 16 to 128, as said below
Outputs:
- new_radiosity: float32 [3, 65536], P(None, 'dev')
Inputs may be any that keep to these rules, and one draw needn't show every extreme that they name: `parent_index`: within each shard's 512 leaves every cluster 0 to 255 is named at least once. The first block_count slots of a device are live, the rest are ignored. For every index of dev exactly one index of grp has 128 live slots; the others have at most 64.
All inputs are finite; a program needn't handle non-finite values.
Results may differ from a plain program's by a relative error of at most 0.0001.
Values sent between devices are 32-bit elements; how exact they have to be, the bound alone decides.
No kernel may reach another device: no remote copies, remote signals or barrier semaphores. Data moves between devices by JAX's collectives and lax.ppermute only.
A program may use at most 64 MiB of HBM per device.

v0:
```python
import jax
import jax.numpy as jnp
from jax import lax
from jax.sharding import Mesh
from jax.sharding import PartitionSpec as P

TILE = 128
DEV = ("dev_0", "dev_1", "dev_2")


batch_slots = 16


def in_order(parts, dim):
    shape = list(parts.shape[1:])
    shape[dim] *= parts.shape[0]
    return jnp.moveaxis(parts, 0, dim).reshape(shape)


def all_blocks(array, axes, order):
    parts = array[None]
    for k in order:
        parts = lax.all_gather(parts, axes[k], axis=0, tiled=True)
    held = [lax.axis_size(axes[k]) for k in reversed(order)]
    parts = parts.reshape(*held, *array.shape)
    turned = sorted(range(len(order)), key=lambda place: order[len(order) - 1 - place])
    return parts.transpose(*turned, *range(len(order), parts.ndim)).reshape(-1, *array.shape)


def gather_axes(array, axes, order, dim):
    return in_order(all_blocks(array, axes, order), dim)


def in_one_piece(arrays, axis, dim, along):
    ends, at = ([], 0)
    for a in arrays[:-1]:
        at += a.shape[along]
        ends.append(at)
    both = jnp.concatenate(arrays, axis=along)
    return tuple(jnp.split(lax.all_gather(both, axis, axis=dim, tiled=True), ends, axis=along))


def from_everyone(array, axis):
    length = lax.axis_size(axis)
    return lax.all_to_all(
        jnp.broadcast_to(array[None], (length, *array.shape)), axis, 0, 0, tiled=True
    )


def taken_together(array, axis):
    return from_everyone(array, axis).sum(axis=0)


def unit_normals(node_angles):
    azimuth = node_angles[0]
    elevation = node_angles[1]
    return jnp.stack(
        [
            jnp.cos(azimuth) * jnp.cos(elevation),
            jnp.sin(azimuth) * jnp.cos(elevation),
            jnp.sin(elevation),
        ]
    )


def tile_irradiance(receivers, sources):
    offsets = [
        sources[axis_id][:, None, :] - receivers[axis_id][:, :, None] for axis_id in range(3)
    ]
    distance_sq = offsets[0] * offsets[0] + offsets[1] * offsets[1] + offsets[2] * offsets[2]
    facing_receiver = (
        receivers[3][:, :, None] * offsets[0]
        + receivers[4][:, :, None] * offsets[1]
        + receivers[5][:, :, None] * offsets[2]
    )
    facing_source = (
        sources[3][:, None, :] * offsets[0]
        + sources[4][:, None, :] * offsets[1]
        + sources[5][:, None, :] * offsets[2]
    )
    source_area = sources[6][:, None, :]
    factor = (
        source_area
        * jnp.maximum(facing_receiver, 0.0)
        * jnp.maximum(-facing_source, 0.0)
        / ((distance_sq + source_area) * (jnp.pi * distance_sq + source_area))
    )
    return jnp.einsum("bij,cbj->bci", factor, sources[7:10], precision=lax.Precision.HIGHEST)


def body(
    leaf_emit,
    leaf_albedo,
    leaf_radiosity,
    leaf_area,
    parent_index,
    node_position,
    node_angles,
    block_receiver,
    block_source,
    block_count,
):
    leaf_count = leaf_area.shape[0]
    node_count = node_position.shape[1]
    cluster_count = node_count - leaf_count
    tile_count = node_count // TILE
    slot_count = block_receiver.shape[1]
    group_count = lax.axis_size("grp")
    normals = unit_normals(node_angles)
    parent_onehot = (
        parent_index[:, None] == jnp.arange(cluster_count, dtype=jnp.int32)[None, :]
    ).astype(jnp.float32)
    cluster_area = jnp.dot(leaf_area, parent_onehot, precision=lax.Precision.HIGHEST)
    weighted = jnp.dot(
        leaf_radiosity * leaf_area[None, :], parent_onehot, precision=lax.Precision.HIGHEST
    )
    cluster_radiosity = weighted / cluster_area[None, :]
    source_pack = jnp.concatenate(
        [
            node_position[:, leaf_count:],
            normals[:, leaf_count:],
            cluster_area[None, :],
            cluster_radiosity,
        ],
        axis=0,
    )
    receiver_pack = jnp.concatenate([node_position, normals], axis=0)
    linked = lax.all_to_all(receiver_pack, DEV, split_axis=1, concat_axis=1, tiled=True)
    receiver_tiles = linked.reshape(6, tile_count, TILE)
    everything = gather_axes(source_pack, DEV, (0, 1, 2), 1)
    source_tiles = everything.reshape(10, -1, TILE)
    all_receivers, all_sources, all_counts = in_one_piece(
        (block_receiver, block_source, block_count), "grp", 0, 1
    )
    counts = all_counts[:, 0]
    ends = jnp.cumsum(counts)
    starts = ends - counts
    total_live = ends[-1]
    my_group = lax.axis_index("grp")
    combined = jnp.arange(slot_count, dtype=jnp.int32) * group_count + my_group
    owner = jnp.sum((combined[:, None] >= ends[None, :]).astype(jnp.int32), axis=1)
    owner = jnp.minimum(owner, group_count - 1)
    slot_index = jnp.clip(combined - jnp.take(starts, owner), 0, slot_count - 1)
    flat_index = owner * slot_count + slot_index
    receiver_ids = jnp.take(all_receivers.reshape(-1), flat_index)
    source_ids = jnp.take(all_sources.reshape(-1), flat_index)
    live_count = jnp.maximum((total_live - my_group + group_count - 1) // group_count, 0)
    step_slots = min(batch_slots, slot_count)

    def add_batch(rounds, totals):
        first = rounds * step_slots
        batch_receivers = lax.dynamic_slice_in_dim(receiver_ids, first, step_slots, 0)
        batch_sources = lax.dynamic_slice_in_dim(source_ids, first, step_slots, 0)
        batch_weight = (first + jnp.arange(step_slots, dtype=jnp.int32) < live_count).astype(
            jnp.float32
        )
        receivers = jnp.take(receiver_tiles, batch_receivers, axis=1)
        sources = jnp.take(source_tiles, batch_sources, axis=1)
        contrib = tile_irradiance(receivers, sources) * batch_weight[:, None, None]
        placement = (
            batch_receivers[:, None] == jnp.arange(tile_count, dtype=jnp.int32)[None, :]
        ).astype(jnp.float32)
        return totals + jnp.einsum(
            "bt,bci->cti", placement, contrib, precision=lax.Precision.HIGHEST
        )

    batch_total = (live_count + step_slots - 1) // step_slots
    totals = lax.fori_loop(0, batch_total, add_batch, jnp.zeros((3, tile_count, TILE), jnp.float32))
    partial_value = totals.reshape(3, node_count)
    summed = taken_together(partial_value, "grp")
    irradiance = lax.all_to_all(summed, DEV, split_axis=1, concat_axis=1, tiled=True)
    pushed = jnp.dot(irradiance[:, leaf_count:], parent_onehot.T, precision=lax.Precision.HIGHEST)
    gathered = irradiance[:, :leaf_count] + pushed
    return leaf_emit + leaf_albedo * gathered


def solution(mesh):
    split = Mesh(
        mesh.devices.reshape(mesh.shape["grp"], 16, 4, 2), ("grp", "dev_0", "dev_1", "dev_2")
    )
    placed = (
        P(None, DEV),
        P(None, DEV),
        P(None, DEV),
        P(DEV),
        P(DEV),
        P(None, DEV),
        P(None, DEV),
        P("grp", DEV),
        P("grp", DEV),
        P("grp", DEV),
    )
    return jax.shard_map(body, mesh=split, in_specs=placed, out_specs=P(None, DEV), check_vma=False)
```

profile of v0, /device:TPU:1, one launch (start us, length us, event | category | flops | bytes accessed | tf_op | source)
XLA Modules:
  0.0 184.8 jit_solution(6144359435645110202)
XLA Ops:
  6.5 1.0 fusion.55
  7.5 0.7 slice.65
  8.2 1.0 fusion.42
  9.2 1.1 convolution_divide_fusion
  10.3 30.5 %all-gather.2 = f32[16,10,256]{2,1,0:T(8,128)S(1)} all-gather(f32[1,10,256]{2,1,0:T(8,128)S(1)} %fusion.49), channel_id=2, replica_groups=mesh['grp'=4,'dev_0'=16,'dev_1'=4,'dev_2'=2] {'dev_0'}, dimensions={0}, use_global_device_ids=true | all-gather | bytes 174080 | tf_op jit(solution)/shard_map/all_gather | solution.py:23
  40.9 11.6 %all_gather.14 = f32[64,10,256]{2,0,1:T(8,128)} all-gather(f32[16,10,256]{2,0,1:T(8,128)S(1)} %copy.41), channel_id=1, replica_groups=mesh['grp'=4,'dev_0'=16,'dev_1'=4,'dev_2'=2] {'dev_1'}, dimensions={0}, use_global_device_ids=true | all-gather | bytes 819200 | tf_op jit(solution)/shard_map/all_gather | solution.py:23
  53.2 1.0 copy.43
  54.2 20.4 %all-to-all-start = ((f32[6,128,6]{2,0,1:T(8,128)}), f32[6,128,6]{2,0,1:T(8,128)S(1)}, u32[]{:S(2)}, u32[]{:S(2)}) async-start(f32[6,128,6]{2,0,1:T(8,128)} %copy.43), calls=%async_computation | async-start | bytes 1048576 | tf_op jit(solution)/shard_map/all_to_all | solution.py:128
  75.3 9.1 %all-gather.1 = s32[4,1,257]{2,1,0:T(1,128)S(1)} all-gather(s32[1,1,257]{2,1,0:T(1,128)S(1)} %add_bitcast_fusion), channel_id=1, replica_groups=mesh['grp'=4,'dev_0'=16,'dev_1'=4,'dev_2'=2] {'grp'}, dimensions={0}, use_global_device_ids=true | all-gather | bytes 5140 | tf_op jit(solution)/shard_map/all_gather | solution.py:40
  84.8 0.7 fusion.60
  85.5 2.6 %compare_select_fusion.2 = s32[128]{0:T(128)S(1)} fusion(s32[128]{0:T(128)S(1)} %convert_reduce_fusion, s32[]{:T(128)} %bitcast.20, s32[]{:T(128)} %bitcast.21, s32[]{:T(128)} %bitcast.23, s32[]{:T(128)} %bitcast.22, s32[]{:T(128)S(6)} %axis_index.15), kind=kLoop, calls=%fused_computation.88 | loop fusion | flops 3328 | bytes 1044 | tf_op jit(solution)/shard_map/jit(_take)/jit(_where)/select_n | solution.py:146
  88.2 1.3 gather_fusion.2
  89.4 1.3 gather_fusion.3
  90.7 2.6 %broadcast_select_fusion = (s32[128]{0:T(128)S(1)}, s32[128]{0:T(128)S(1)}) fusion(s32[128]{0:T(128)S(1)} %gather_fusion.3, s32[128]{0:T(128)S(1)} %gather_fusion.2, s32[]{:T(128)} %bitcast.23, s32[]{:T(128)} %bitcast.22, s32[]{:T(128)} %bitcast.21, s32[]{:T(128)} %bitcast.20, s32[]{:T(128)S(6)} %axis_index.15, s32[128]{0:T(128)S(1)} %convert_reduce_fusion), kind=kLoop, calls=%fused_computation.105 | loop fusion | flops 3968 | bytes 2580 | tf_op jit(solution)/shard_map/jit(_take)/select_n | solution.py:145
  94.5 10.9 %all-to-all-done = f32[6,128,6]{2,0,1:T(8,128)S(1)} async-done(((f32[6,128,6]{2,0,1:T(8,128)}), f32[6,128,6]{2,0,1:T(8,128)S(1)}, u32[]{:S(2)}, u32[]{:S(2)}) %all-to-all-start) | async-done | bytes 18464 | tf_op jit(solution)/shard_map/all_to_all | solution.py:128
  105.9 2.3 %copy.58 = f32[2,4,16,10,256]{4,0,1,2,3:T(2,128)S(1)} copy(f32[2,4,16,10,256]{4,2,1,0,3:T(8,128)} %bitcast.104) | data formatting | bytes 2621440 | tf_op jit(solution)/shard_map/reshape | solution.py:25
  108.2 0.9 reshape.100
  109.2 0.8 copy.45
  110.0 22.2 %while.10 = (s32[]{:T(128)}, f32[3,6,128]{2,1,0:T(8,128)S(1)}, s32[]{:T(128)}, s32[128]{0:T(128)S(1)}, f32[10,256,128]{2,0,1:T(8,128)S(1)}, /*index=5*/s32[128]{...) while((s32[]{:T(128)}, f32[3,6,128]{2,1,0:T(8,128)S(1)}, ...), condition=%wide.region_3.5_spmd, body=%wide.region_2.4_spmd.sunk | while | flops 17263236 | bytes 953843 | solution.py:168
  111.0 0.6 gather_fusion
  111.7 3.8 %convolution_multiply_fusion.2 = f32[16,3,128]{2,1,0:T(4,128)S(1)} fusion(f32[16,128]{1,0:T(8,128)S(1)} %bitcast.107, f32[16,128]{1,0:T(8,128)S(1)} %bitcast.108, f32[16,128]{1,0:T(8,128)S(1)} %bitcast.109, f32[16,128]{1,0:T(8,128)S(1)} %bitcast.114, f32[16,128]{1,0:T(8,128)S(1)} %bitcast.110, f32[16,128]{1,0:T(8,128)S(1)} %bitcast.115, ...), kind=kOutput, calls=%fused_computation.13.clone.1 | convolution fusion | flops 16783360 | bytes 164352 | tf_op jit(solution)/shard_map/while/body/bij,cbj->bci/dot_general | solution.py:88
  115.7 0.6 gather_fusion.1
  116.5 0.6 gather_fusion
  117.2 3.8 %convolution_multiply_fusion.2 = f32[16,3,128]{2,1,0:T(4,128)S(1)} fusion(f32[16,128]{1,0:T(8,128)S(1)} %bitcast.107, f32[16,128]{1,0:T(8,128)S(1)} %bitcast.108, f32[16,128]{1,0:T(8,128)S(1)} %bitcast.109, f32[16,128]{1,0:T(8,128)S(1)} %bitcast.114, f32[16,128]{1,0:T(8,128)S(1)} %bitcast.110, f32[16,128]{1,0:T(8,128)S(1)} %bitcast.115, ...), kind=kOutput, calls=%fused_computation.13.clone.1 | convolution fusion | flops 16783360 | bytes 164352 | tf_op jit(solution)/shard_map/while/body/bij,cbj->bci/dot_general | solution.py:88
  121.2 0.6 gather_fusion.1
  122.0 0.6 gather_fusion
  122.7 3.8 %convolution_multiply_fusion.2 = f32[16,3,128]{2,1,0:T(4,128)S(1)} fusion(f32[16,128]{1,0:T(8,128)S(1)} %bitcast.107, f32[16,128]{1,0:T(8,128)S(1)} %bitcast.108, f32[16,128]{1,0:T(8,128)S(1)} %bitcast.109, f32[16,128]{1,0:T(8,128)S(1)} %bitcast.114, f32[16,128]{1,0:T(8,128)S(1)} %bitcast.110, f32[16,128]{1,0:T(8,128)S(1)} %bitcast.115, ...), kind=kOutput, calls=%fused_computation.13.clone.1 | convolution fusion | flops 16783360 | bytes 164352 | tf_op jit(solution)/shard_map/while/body/bij,cbj->bci/dot_general | solution.py:88
  126.8 0.6 gather_fusion.1
  128.3 3.8 %convolution_multiply_fusion.2 = f32[16,3,128]{2,1,0:T(4,128)S(1)} fusion(f32[16,128]{1,0:T(8,128)S(1)} %bitcast.107, f32[16,128]{1,0:T(8,128)S(1)} %bitcast.108, f32[16,128]{1,0:T(8,128)S(1)} %bitcast.109, f32[16,128]{1,0:T(8,128)S(1)} %bitcast.114, f32[16,128]{1,0:T(8,128)S(1)} %bitcast.110, f32[16,128]{1,0:T(8,128)S(1)} %bitcast.115, ...), kind=kOutput, calls=%fused_computation.13.clone.1 | convolution fusion | flops 16783360 | bytes 164352 | tf_op jit(solution)/shard_map/while/body/bij,cbj->bci/dot_general | solution.py:88
  132.3 8.2 %all_to_all.23 = f32[4,3,768]{2,1,0:T(4,128)S(1)} all-to-all(f32[4,3,768]{2,1,0:T(4,128)S(1)} %broadcast_in_dim.66), channel_id=1, replica_groups=mesh['grp'=4,'dev_0'=16,'dev_1'=4,'dev_2'=2] {'grp'}, dimensions={0} | all-to-all | bytes 73728 | tf_op jit(solution)/shard_map/all_to_all | solution.py:45
  140.8 35.9 %all_to_all.24 = f32[3,128,6]{2,0,1:T(4,128)S(1)} all-to-all(f32[3,128,6]{2,0,1:T(4,128)S(1)} %copy.48), channel_id=1, replica_groups=mesh['grp'=4,'dev_0'=16,'dev_1'=4,'dev_2'=2] {'dev_0','dev_1','dev_2'}, dimensions={1} | all-to-all | bytes 18432 | tf_op jit(solution)/shard_map/all_to_all | solution.py:171
  176.9 1.0 fusion.41
  (87 shorter events, 6.1 us)
Async XLA Ops:
  6.5 46.0 %copy-start = (f32[3,768]{1,0:T(4,128)S(1)}, f32[3,768]{1,0:T(4,128)}, u32[]{:S(2)}) copy-start(f32[3,768]{1,0:T(4,128)} %param.19) | copy-start | bytes 27652
  6.5 99.3 %all-gather.5.cloned.1.call-start = ((), (), s32[]{:S(2)}) async-start(), calls=%async_computation.3 | async-start | bytes 1966080 | tf_op jit(solution)/shard_map/all_gather | solution.py:23
  53.1 22.2 %copy-start.1 = (s32[1,128]{1,0:T(1,128)S(1)}, s32[1,128]{1,0:T(1,128)}, u32[]{:S(2)}) copy-start(s32[1,128]{1,0:T(1,128)} %param.22) | copy-start | bytes 1540
  53.1 22.2 %copy-start.2 = (s32[1,128]{1,0:T(1,128)S(1)}, s32[1,128]{1,0:T(1,128)}, u32[]{:S(2)}) copy-start(s32[1,128]{1,0:T(1,128)} %param.21) | copy-start | bytes 1540
  54.2 51.2 %all-to-all-start = ((f32[6,128,6]{2,0,1:T(8,128)}), f32[6,128,6]{2,0,1:T(8,128)S(1)}, u32[]{:S(2)}, u32[]{:S(2)}) async-start(f32[6,128,6]{2,0,1:T(8,128)} %copy.43), calls=%async_computation | async-start | bytes 1048576 | tf_op jit(solution)/shard_map/all_to_all | solution.py:128
  132.2 44.7 %copy-start.3 = (f32[3,512]{1,0:T(4,128)S(1)}, f32[3,512]{1,0:T(4,128)}, u32[]{:S(2)}) copy-start(f32[3,512]{1,0:T(4,128)} %param.14) | copy-start | bytes 18436
  132.2 44.7 %copy-start.4 = (f32[3,512]{1,0:T(4,128)S(1)}, f32[3,512]{1,0:T(4,128)}, u32[]{:S(2)}) copy-start(f32[3,512]{1,0:T(4,128)} %param.15) | copy-start | bytes 18436
  132.2 44.7 %copy-start.5 = (s32[512]{0:T(512)S(1)}, s32[512]{0:T(512)}, u32[]{:S(2)}) copy-start(s32[512]{0:T(512)} %param.18) | copy-start | bytes 6148
Sparse Core Ops, SparseCore 0:
  52.6 26.4 all-gather.4
where the time goes:
time: 186 us; the launch traced here: 185 us
  blocking collectives  95.3 us (51%)
  starting transfers between devices  20.4 us (11%)
  matrix products  18.7 us (10%)
  local copies, waits for them, and re-layouts  16.1 us (9%)
  between operations  15 us (8%)
  waiting for transfers between devices  11 us (6%)
  other arithmetic  7.96 us (4%)
    all_gather x2, blocking collectives, all_blocks(): parts = lax.all_gather(parts, axes[k], axis=0, tiled=True)  42.1 us
    all_to_all x1, blocking collectives, body(): lax.all_to_all(summed, DEV, split_axis=1, concat_axis=1, tiled=True)  35.9 us
    all_to_all x1, starting transfers between devices, body(): lax.all_to_all(receiver_pack, DEV, split_axis=1, concat_axis=1, tiled=True)  20.4 us
    dot_general x4, matrix products, tile_irradiance(): jnp.einsum('bij,cbj->bci', factor, sources[7:10], precision=lax.Precision...  15.1 us
    all_to_all x1, waiting for transfers between devices, body(): lax.all_to_all(receiver_pack, DEV, split_axis=1, concat_axis=1, tiled=True)  10.9 us
    all_gather x1, blocking collectives, in_one_piece(): lax.all_gather(both, axis, axis=dim, tiled=True)  9.14 us
    all_to_all x1, blocking collectives, from_everyone(): lax.all_to_all(jnp.broadcast_to(array[None], (length, *array.shape)), axi...  8.2 us
  transfers between devices with their start and end apart: 2, of which 1 were waited for; matrix products, arithmetic and copies ran while one was open for 6% of the time, Pallas kernels for 0%

commit v1 on v0

v1 whole, which is shorter than its diff:
```python
import functools
import math

import jax
import jax.numpy as jnp
from jax import lax
from jax.experimental import pallas as pl
from jax.experimental.pallas import tpu as pltpu
from jax.sharding import Mesh
from jax.sharding import PartitionSpec as P

TILE = 128
DEV = ("dev_0", "dev_1", "dev_2")
QUAD = 4
PACK = 20
FIELDS = 9
OFFSETS = 248
EMPTY = 40
EXACT = lax.Precision.HIGHEST
NT_DIMS = (((1,), (1,)), ((), ()))


def pack_kernel(
    radiosity, area, parent, position, angles, receiver, source, count, pack_out, nodes_out
):
    leaf_count = area.shape[1]
    node_count = position.shape[1]
    cluster_count = node_count - leaf_count
    azimuth = angles[0:1, :]
    elevation = angles[1:2, :]
    cos_e = jnp.cos(elevation)
    nodes_out[0:3, :] = position[...]
    nodes_out[3:4, :] = jnp.cos(azimuth) * cos_e
    nodes_out[4:5, :] = jnp.sin(azimuth) * cos_e
    nodes_out[5:6, :] = jnp.sin(elevation)
    nodes_out[6:8, :] = jnp.zeros((2, node_count), jnp.float32)
    clusters = lax.broadcasted_iota(jnp.int32, (cluster_count, leaf_count), 0)
    onehot = (clusters == parent[...]).astype(jnp.float32)
    leaf_area = area[...]
    values = jnp.concatenate(
        [leaf_area, radiosity[...] * leaf_area, jnp.zeros((4, leaf_count), jnp.float32)], axis=0
    )
    sums = lax.dot_general(
        values, onehot, NT_DIMS, precision=EXACT, preferred_element_type=jnp.float32
    )
    cluster_area = sums[0:1, :]
    cluster_radiosity = sums[1:4, :] / cluster_area
    scaled = nodes_out[3:6, leaf_count:] * (cluster_area * (-1.0 / math.pi))
    slots = receiver.shape[1]
    tiles = lax.broadcasted_iota(jnp.int32, (8, slots), 0)
    lanes = lax.broadcasted_iota(jnp.int32, (8, slots), 1)
    live = lanes < count[...]
    member = jnp.where((tiles == receiver[...]) & live, 1.0, 0.0)
    before = (
        lax.broadcasted_iota(jnp.int32, (slots, slots), 0)
        < lax.broadcasted_iota(jnp.int32, (slots, slots), 1)
    ).astype(jnp.float32)
    place = jnp.dot(member, before, preferred_element_type=jnp.float32)
    held = jnp.sum(member, axis=1, keepdims=True)
    quads = jnp.broadcast_to(jnp.floor((held + (QUAD - 1)) * (1.0 / QUAD)), (8, slots))
    first = jnp.zeros((8, slots), jnp.float32)
    for t in range(7):
        first = first + jnp.where(tiles > t, quads[t : t + 1, :], 0.0)
    spot = jnp.sum(member * (first * QUAD + place), axis=0, keepdims=True)
    alive = jnp.sum(member, axis=0, keepdims=True)
    spot = jnp.where(alive > 0.0, spot, -1.0).astype(jnp.int32)
    to_spot = (lax.broadcasted_iota(jnp.int32, (2 * slots, slots), 0) == spot).astype(jnp.float32)
    entries = jnp.broadcast_to((source[...] + 1).astype(jnp.float32), (8, slots))
    ordered = lax.dot_general(entries, to_spot, NT_DIMS, preferred_element_type=jnp.float32)
    offsets = jnp.sum(
        jnp.where(lanes == OFFSETS - TILE + tiles, first, 0.0), axis=0, keepdims=True
    )
    rows = []
    for half in range(2):
        cols = slice(half * TILE, half * TILE + TILE)
        at = slice(leaf_count + half * TILE, leaf_count + half * TILE + TILE)
        rows += [position[:, at], scaled[:, cols], cluster_radiosity[:, cols]]
    rows += [ordered[0:1, :TILE], ordered[0:1, TILE:] + offsets]
    packed = jnp.concatenate(rows, axis=0)
    for peer in range(pack_out.shape[0]):
        pack_out[peer] = packed


def gather_kernel(
    where_ref,
    sources_hbm,
    nodes_ref,
    parent_ref,
    out_ref,
    sources,
    area,
    area_pi,
    receivers,
    totals,
    table_vmem,
    table,
    sem,
    table_sem,
    *,
    sizes,
):
    shard_z, shard_y, shard_c = sizes
    shards = shard_z * shard_y * shard_c
    node_count = nodes_ref.shape[1]
    per_peer = node_count // shards
    null_row = shards * PACK
    copy = pltpu.make_async_copy(sources_hbm, sources.at[pl.ds(0, null_row)], sem)
    copy.start()
    for chunk in range(node_count // TILE):
        at = slice(chunk * TILE, chunk * TILE + TILE)
        turned = nodes_ref[:, at].T
        for field in range(6):
            receivers[field, at, :] = jnp.broadcast_to(turned[:, field : field + 1], (TILE, TILE))
    for field in range(6):
        receivers[field, node_count : node_count + 8, :] = jnp.zeros((8, TILE), jnp.float32)
    copy.wait()
    sources[null_row : null_row + 16, :] = jnp.zeros((16, TILE), jnp.float32)
    area[null_row : null_row + 8, :] = jnp.ones((8, TILE), jnp.float32)
    area_pi[null_row : null_row + 8, :] = jnp.ones((8, TILE), jnp.float32)
    for half in range(2):
        base = half * FIELDS
        bx, by, bz = (sources[pl.ds(base + 3 + a, shards, stride=PACK), :] for a in range(3))
        length = jnp.sqrt(bx * bx + by * by + bz * bz)
        area_pi[pl.ds(base, shards, stride=PACK), :] = length
        area[pl.ds(base, shards, stride=PACK), :] = length * math.pi
    column = lax.broadcasted_iota(jnp.int32, (shard_z, TILE), 1)
    per_c = shard_y * shard_z

    def source_row(entry):
        tile = entry - 1
        half = tile & 1
        owner = tile >> 1
        arrival = (
            (owner & (shard_c - 1)) * per_c
            + ((owner // shard_c) & (shard_y - 1)) * shard_z
            + owner // (shard_c * shard_y)
        )
        return jnp.where(entry == 0, null_row, arrival * PACK + half * FIELDS)

    for c in range(shard_c):
        for y in range(shard_y):
            begin = (c * per_c + y * shard_z) * PACK + 2 * FIELDS
            low = sources[pl.ds(begin, shard_z, stride=PACK), :].astype(jnp.int32)
            high = sources[pl.ds(begin + 1, shard_z, stride=PACK), :].astype(jnp.int32)
            rows = pl.ds(y * shard_c + c, shard_z, stride=shard_y * shard_c)
            table_vmem[0, rows, :] = source_row(low)
            table_vmem[1, rows, :] = jnp.where(column < OFFSETS - TILE, source_row(high), high)
    extra = lax.broadcasted_iota(jnp.int32, (8, TILE), 1)
    table_vmem[0, shards : shards + 8, :] = jnp.full((8, TILE), null_row, jnp.int32)
    table_vmem[1, shards : shards + 8, :] = jnp.where(extra < OFFSETS - TILE, null_row, 0)
    to_smem = pltpu.make_async_copy(table_vmem, table, table_sem)
    to_smem.start()
    to_smem.wait()

    first_tile = where_ref[0] * per_peer // TILE
    last_tile = (where_ref[0] * per_peer + per_peer - 1) // TILE

    def run_pass(which, tile):
        def enter(shard):
            begin = table[1, shard, OFFSETS - TILE + tile]
            end = table[1, shard, OFFSETS - TILE + tile + 1]
            empty = begin == end
            return jnp.where(empty, EMPTY, begin), jnp.where(empty, EMPTY + 1, end)

        def one_quad(state):
            shard, quad, end, keep, acc = state
            node = shard * per_peer
            rec = [receivers[field, pl.ds(node, 8), :] for field in range(6)]
            acc = [a * keep for a in acc]
            plane = (quad * QUAD) // TILE
            spot = (quad * QUAD) % TILE
            for u in range(QUAD):
                row = table[plane, shard, spot + u]
                src = [sources[pl.ds(row + f, 1), :] for f in range(FIELDS)]
                d = [src[a] - rec[a] for a in range(3)]
                r2 = d[0] * d[0] + d[1] * d[1] + d[2] * d[2]
                toward = rec[3] * d[0] + rec[4] * d[1] + rec[5] * d[2]
                back = src[3] * d[0] + src[4] * d[1] + src[5] * d[2]
                top = jnp.maximum(toward, 0.0) * jnp.maximum(back, 0.0)
                bottom = (r2 + area[pl.ds(row, 1), :]) * (r2 + area_pi[pl.ds(row, 1), :])
                factor = top / bottom
                acc = [acc[c] + factor * src[6 + c] for c in range(3)]
            for c in range(3):
                totals[which, c, pl.ds(node, 8), :] = acc[c]
            quad = quad + 1
            done = quad >= end
            shard = jnp.where(done, shard + 1, shard)
            begin_next, end_next = enter(shard)
            quad = jnp.where(done, begin_next, quad)
            end = jnp.where(done, end_next, end)
            keep = jnp.where(done, 0.0, 1.0)
            return shard, quad, end, keep, acc

        def step(state):
            for _ in range(2):
                state = one_quad(state)
            return state

        begin, end = enter(0)
        zero = jnp.zeros((8, TILE), jnp.float32)
        lax.while_loop(
            lambda state: state[0] < shards,
            step,
            (jnp.int32(0), begin, end, jnp.float32(0.0), [zero, zero, zero]),
        )

    run_pass(0, first_tile)
    straddles = last_tile > first_tile

    @pl.when(straddles)
    def _():
        run_pass(1, last_tile)
        split = last_tile * TILE - where_ref[0] * per_peer
        within = lax.broadcasted_iota(jnp.int32, (node_count, TILE), 0) % per_peer
        for c in range(3):
            totals[0, c, 0:node_count, :] = jnp.where(
                within >= split, totals[1, c, 0:node_count, :], totals[0, c, 0:node_count, :]
            )

    ones = jnp.ones((8, TILE), jnp.float32)
    irradiance = jnp.concatenate(
        [
            lax.dot_general(
                ones,
                totals[0, c, 0:node_count, :],
                NT_DIMS,
                precision=EXACT,
                preferred_element_type=jnp.float32,
            )[0:1, :]
            for c in range(3)
        ]
        + [jnp.zeros((5, node_count), jnp.float32)],
        axis=0,
    )
    leaf_count = parent_ref.shape[1]
    cluster_count = node_count - leaf_count
    clusters = lax.broadcasted_iota(jnp.int32, (cluster_count, leaf_count), 0)
    onehot = (clusters == parent_ref[...]).astype(jnp.float32)
    pushed = jnp.dot(
        irradiance[:, leaf_count:], onehot, precision=EXACT, preferred_element_type=jnp.float32
    )
    gathered = (irradiance[:, :leaf_count] + pushed)[0:3, :]
    for group in range(out_ref.shape[0]):
        out_ref[group] = gathered


def body(
    leaf_emit,
    leaf_albedo,
    leaf_radiosity,
    leaf_area,
    parent_index,
    node_position,
    node_angles,
    block_receiver,
    block_source,
    block_count,
):
    leaf_count = leaf_area.shape[0]
    node_count = node_position.shape[1]
    sizes = tuple(lax.axis_size(axis) for axis in DEV)
    shards = sizes[0] * sizes[1] * sizes[2]
    groups = lax.axis_size("grp")
    parent = parent_index[None, :]
    vmem = pl.BlockSpec(memory_space=pltpu.VMEM)
    pack, nodes = pl.pallas_call(
        pack_kernel,
        out_shape=(
            jax.ShapeDtypeStruct((sizes[0], PACK, TILE), jnp.float32),
            jax.ShapeDtypeStruct((8, node_count), jnp.float32),
        ),
        in_specs=[vmem] * 8,
        out_specs=(vmem, vmem),
        name="pack",
    )(
        leaf_radiosity,
        leaf_area[None, :],
        parent,
        node_position,
        node_angles,
        block_receiver,
        block_source,
        block_count,
    )
    held = pack.reshape(sizes[0], PACK // 4, 4, TILE)
    held = lax.all_to_all(held, DEV[0], 0, 0, tiled=True)
    for axis, size in zip(DEV[1:], sizes[1:]):
        held = held.reshape(-1, 4, TILE)
        held = lax.all_to_all(
            jnp.broadcast_to(held[None], (size, *held.shape)), axis, 0, 0, tiled=True
        )
    everything = held.reshape(shards * PACK, TILE)
    where = lax.axis_index(DEV).astype(jnp.int32).reshape(1)
    rows = shards * PACK
    partial = pl.pallas_call(
        functools.partial(gather_kernel, sizes=sizes),
        out_shape=jax.ShapeDtypeStruct((groups, 3, leaf_count), jnp.float32),
        in_specs=[
            pl.BlockSpec(memory_space=pltpu.SMEM),
            pl.BlockSpec(memory_space=pl.ANY),
            vmem,
            vmem,
        ],
        out_specs=vmem,
        scratch_shapes=[
            pltpu.VMEM((rows + 16, TILE), jnp.float32),
            pltpu.VMEM((rows + 16, TILE), jnp.float32),
            pltpu.VMEM((rows + 16, TILE), jnp.float32),
            pltpu.VMEM((6, node_count + 8, TILE), jnp.float32),
            pltpu.VMEM((2, 3, node_count + 8, TILE), jnp.float32),
            pltpu.VMEM((2, shards + 8, TILE), jnp.int32),
            pltpu.SMEM((2, shards + 8, TILE), jnp.int32),
            pltpu.SemaphoreType.DMA(()),
            pltpu.SemaphoreType.DMA(()),
        ],
        compiler_params=pltpu.CompilerParams(vmem_limit_bytes=40 * 1024 * 1024),
        name="gather",
    )(where, everything, nodes, parent)
    gathered = lax.all_to_all(partial, "grp", 0, 0, tiled=True).sum(axis=0)
    return leaf_emit + leaf_albedo * gathered


def solution(mesh):
    split = Mesh(
        mesh.devices.reshape(mesh.shape["grp"], 16, 4, 2), ("grp", "dev_0", "dev_1", "dev_2")
    )
    placed = (
        P(None, DEV),
        P(None, DEV),
        P(None, DEV),
        P(DEV),
        P(DEV),
        P(None, DEV),
        P(None, DEV),
        P("grp", DEV),
        P("grp", DEV),
        P("grp", DEV),
    )
    return jax.shard_map(body, mesh=split, in_specs=placed, out_specs=P(None, DEV), check_vma=False)
```

time: 186 us -> 90.2 us (0.48)
  the two profiles are of different devices: /device:TPU:1 before, /device:TPU:81 now
where the time goes in v1:
time: 90.2 us; the launch traced here: 89.9 us
  blocking collectives  44.8 us (50%)
  Pallas kernels  32.4 us (36%)
  waiting for transfers between devices  4.95 us (5%)
  starting transfers between devices  4.24 us (5%)
  local copies, waits for them, and re-layouts  2.14 us (2%)
    pallas_call x1, Pallas kernels, body(): pl.pallas_call(functools.partial(gather_kernel, sizes=sizes), out_shape=j...  30.2 us
    all_to_all x1, blocking collectives, body(): held = lax.all_to_all(held, DEV[0], 0, 0, tiled=True)  26.9 us
    all_to_all x1, blocking collectives, body(): lax.all_to_all(jnp.broadcast_to(held[None], (size, *held.shape)), axis, 0...  9.04 us
    all_to_all x1, blocking collectives, body(): gathered = lax.all_to_all(partial, 'grp', 0, 0, tiled=True).sum(axis=0)  8.84 us
    all_to_all x1, waiting for transfers between devices, body(): lax.all_to_all(jnp.broadcast_to(held[None], (size, *held.shape)), axis, 0...  4.95 us
    all_to_all x1, starting transfers between devices, body(): lax.all_to_all(jnp.broadcast_to(held[None], (size, *held.shape)), axis, 0...  4.24 us
    pallas_call x1, Pallas kernels, body(): pl.pallas_call(pack_kernel, out_shape=(jax.ShapeDtypeStruct((sizes[0], PA...  2.21 us
  transfers between devices with their start and end apart: 1, of which 1 were waited for; matrix products, arithmetic and copies ran while one was open for 0% of the time, Pallas kernels for 0%

profile of v1, /device:TPU:81, one launch (start us, length us, event | category | flops | bytes accessed | tf_op | source)
XLA Modules:
  0.0 89.9 jit_solution(16265988047511242557)
XLA Ops:
  0.7 2.2 %pack.1 = (f32[16,20,128]{2,1,0:T(8,128)}, f32[8,768]{1,0:T(8,128)}) custom-call(f32[3,512]{1,0:T(4,128)} %radiosity.1, f32[1,512]{1,0:T(1,128)} %bitcast.13, s32[1,512]{1,0:T(1,128)} %bitcast.8, f32[3,768]{1,0:T(4,128)} %position.1, f32[2,768]{1,0:T(2,128)} %angles.1, s32[1,128]{1,0:T(1,128)} %receiver.1, s32[1,128]{1,0:T(1,128)} %source.1, ...), custom_call_target="tpu_custom_call" | custom-call | tf_op jit(solution)/shard_map/pack/pallas_call | solution.py:266
  2.9 1.0 %copy.14 = f32[16,20,128]{2,0,1:T(8,128)S(1)} copy(f32[16,20,128]{2,1,0:T(8,128)} %get-tuple-element.7) | data formatting | bytes 327680 | tf_op jit(solution)/shard_map/pack/pallas_call | solution.py:266
  3.8 0.1 copy.15
  3.9 26.9 %all_to_all.20 = f32[16,5,4,128]{3,2,1,0:T(4,128)S(1)} all-to-all(f32[16,5,4,128]{3,2,1,0:T(4,128)S(1)} %copy.15), channel_id=1, replica_groups=mesh['grp'=4,'dev_0'=16,'dev_1'=4,'dev_2'=2] {'dev_0'}, dimensions={0} | all-to-all | bytes 327680 | tf_op jit(solution)/shard_map/all_to_all | solution.py:286
  30.8 0.9 %broadcast_in_dim.23 = f32[4,80,4,128]{3,2,1,0:T(4,128)} broadcast(f32[80,4,128]{2,1,0:T(4,128)S(1)} %bitcast.12), dimensions={1,2,3} | broadcast | bytes 819200 | tf_op jit(solution)/shard_map/broadcast_in_dim | solution.py:290
  31.7 4.2 %all-to-all-start.1 = ((f32[4,80,4,128]{3,2,1,0:T(4,128)}), f32[4,80,4,128]{3,2,1,0:T(4,128)S(1)}, u32[]{:S(2)}, u32[]{:S(2)}) async-start(f32[4,80,4,128]{3,2,1,0:T(4,128)} %broadcast_in_dim.23), calls=%async_computation.1 | async-start | bytes 1310720 | tf_op jit(solution)/shard_map/all_to_all | solution.py:289
  36.0 5.0 %all-to-all-done.1 = f32[4,80,4,128]{3,2,1,0:T(4,128)S(1)} async-done(((f32[4,80,4,128]{3,2,1,0:T(4,128)}), f32[4,80,4,128]{3,2,1,0:T(4,128)S(1)}, u32[]{:S(2)}, u32[]{:S(2)}) %all-to-all-start.1) | async-done | bytes 655392 | tf_op jit(solution)/shard_map/all_to_all | solution.py:289
  40.9 0.2 broadcast_in_dim.25
  41.1 0.0 copy-start
  41.1 0.0 copy-start.1
  41.1 9.0 %all_to_all.21 = f32[2,320,4,128]{3,2,1,0:T(4,128)S(1)} all-to-all(f32[2,320,4,128]{3,2,1,0:T(4,128)S(1)} %broadcast_in_dim.25), channel_id=1, replica_groups=mesh['grp'=4,'dev_0'=16,'dev_1'=4,'dev_2'=2] {'dev_2'}, dimensions={0} | all-to-all | bytes 2621440 | tf_op jit(solution)/shard_map/all_to_all | solution.py:289
  50.2 0.0 copy-start.2
  50.2 0.0 copy-start.3
  50.2 0.0 copy-done
  50.2 0.0 copy-done.1
  50.2 30.2 %gather.1 = f32[4,3,512]{2,1,0:T(4,128)S(1)} custom-call(s32[1]{0:T(128)} %bitcast.where_ref, f32[2560,128]{1,0:T(8,128)S(1)} %bitcast.7, f32[8,768]{1,0:T(8,128)S(1)} %copy-done, s32[1,512]{1,0:T(1,128)S(1)} %bitcast.9), custom_call_target="tpu_custom_call" | custom-call | tf_op jit(solution)/shard_map/gather/pallas_call | solution.py:295
  80.4 8.8 %all_to_all.22 = f32[4,3,512]{2,1,0:T(4,128)S(1)} all-to-all(f32[4,3,512]{2,1,0:T(4,128)S(1)} %gather.1), channel_id=1, replica_groups=mesh['grp'=4,'dev_0'=16,'dev_1'=4,'dev_2'=2] {'grp'}, dimensions={0} | all-to-all | bytes 49152 | tf_op jit(solution)/shard_map/all_to_all | solution.py:319
  89.2 0.0 copy-done.2
  89.2 0.0 copy-done.3
  89.2 0.6 multiply_add_fusion
  (1 shorter events, 0.0 us)
Async XLA Ops:
  31.7 9.2 %all-to-all-start.1 = ((f32[4,80,4,128]{3,2,1,0:T(4,128)}), f32[4,80,4,128]{3,2,1,0:T(4,128)S(1)}, u32[]{:S(2)}, u32[]{:S(2)}) async-start(f32[4,80,4,128]{3,2,1,0:T(4,128)} %broadcast_in_dim.23), calls=%async_computation.1 | async-start | bytes 1310720 | tf_op jit(solution)/shard_map/all_to_all | solution.py:289
  41.1 9.1 %copy-start = (f32[8,768]{1,0:T(8,128)S(1)}, f32[8,768]{1,0:T(8,128)}, u32[]{:S(2)}) copy-start(f32[8,768]{1,0:T(8,128)} %get-tuple-element.8.nodes_ref) | copy-start | bytes 73732
  41.1 9.1 %copy-start.1 = (s32[512]{0:T(512)S(1)}, s32[512]{0:T(512)}, u32[]{:S(2)}) copy-start(s32[512]{0:T(512)} %param.14) | copy-start | bytes 6148
  50.2 39.1 %copy-start.2 = (f32[3,512]{1,0:T(4,128)S(1)}, f32[3,512]{1,0:T(4,128)}, u32[]{:S(2)}) copy-start(f32[3,512]{1,0:T(4,128)} %param.10) | copy-start | bytes 18436
  50.2 39.1 %copy-start.3 = (f32[3,512]{1,0:T(4,128)S(1)}, f32[3,512]{1,0:T(4,128)}, u32[]{:S(2)}) copy-start(f32[3,512]{1,0:T(4,128)} %param.11) | copy-start | bytes 18436

commit v2 on v1

v2 whole, which is shorter than its diff:
```python
import functools
import math

import jax
import jax.numpy as jnp
from jax import lax
from jax.experimental import pallas as pl
from jax.experimental.pallas import tpu as pltpu
from jax.sharding import Mesh
from jax.sharding import PartitionSpec as P

TILE = 128
DEV = ("dev_0", "dev_1", "dev_2")
QUAD = 4
STEP = 4
PACK = 20
FIELDS = 9
SOURCE = 16
OFFSETS = 248
EMPTY = 40
START = 254
STOP = 255
HEAD = 32
EXACT = lax.Precision.HIGHEST
NT_DIMS = (((1,), (1,)), ((), ()))


def lane_rows(array):
    return [array[:, at : at + TILE] for at in range(0, array.shape[1], TILE)]


def pack_kernel(
    radiosity, area, parent, position, angles, receiver, source, count, pack_out, local_out
):
    leaf_count = area.shape[1]
    node_count = position.shape[1]
    cluster_count = node_count - leaf_count
    azimuth = angles[0:1, :]
    elevation = angles[1:2, :]
    cos_e = jnp.cos(elevation)
    nodes = [position[a : a + 1, :] for a in range(3)]
    nodes += [jnp.cos(azimuth) * cos_e, jnp.sin(azimuth) * cos_e, jnp.sin(elevation)]
    clusters = lax.broadcasted_iota(jnp.int32, (cluster_count, leaf_count), 0)
    onehot = (clusters == parent[...]).astype(jnp.float32)
    leaf_area = area[...]
    values = jnp.concatenate(
        [leaf_area, radiosity[...] * leaf_area, jnp.zeros((4, leaf_count), jnp.float32)], axis=0
    )
    sums = lax.dot_general(
        values, onehot, NT_DIMS, precision=EXACT, preferred_element_type=jnp.float32
    )
    cluster_area = sums[0:1, :]
    cluster_radiosity = sums[1:4, :] / cluster_area
    scale = cluster_area * (-1.0 / math.pi)
    slots = receiver.shape[1]
    tiles = lax.broadcasted_iota(jnp.int32, (8, slots), 0)
    lanes = lax.broadcasted_iota(jnp.int32, (8, slots), 1)
    live = lanes < count[...]
    member = jnp.where((tiles == receiver[...]) & live, 1.0, 0.0)
    before = (
        lax.broadcasted_iota(jnp.int32, (slots, slots), 0)
        < lax.broadcasted_iota(jnp.int32, (slots, slots), 1)
    ).astype(jnp.float32)
    place = jnp.dot(member, before, preferred_element_type=jnp.float32)
    held = jnp.sum(member, axis=1, keepdims=True)
    quads = jnp.broadcast_to(jnp.floor((held + (QUAD - 1)) * (1.0 / QUAD)), (8, slots))
    first = jnp.zeros((8, slots), jnp.float32)
    for t in range(7):
        first = first + jnp.where(tiles > t, quads[t : t + 1, :], 0.0)
    spot = jnp.sum(member * (first * QUAD + place), axis=0, keepdims=True)
    alive = jnp.sum(member, axis=0, keepdims=True)
    spot = jnp.where(alive > 0.0, spot, -1.0).astype(jnp.int32)
    to_spot = (lax.broadcasted_iota(jnp.int32, (2 * slots, slots), 0) == spot).astype(jnp.float32)
    entries = jnp.broadcast_to((source[...] + 1).astype(jnp.float32), (8, slots))
    ordered = lax.dot_general(entries, to_spot, NT_DIMS, preferred_element_type=jnp.float32)
    offsets = jnp.sum(
        jnp.where(lanes == OFFSETS - TILE + tiles, first, 0.0), axis=0, keepdims=True
    )
    rows = []
    for half in range(cluster_count // TILE):
        cols = slice(half * TILE, half * TILE + TILE)
        at = slice(leaf_count + half * TILE, leaf_count + half * TILE + TILE)
        rows += [nodes[a][:, at] for a in range(3)]
        rows += [nodes[a][:, at] * scale[:, cols] for a in range(3, 6)]
        rows += [cluster_radiosity[c : c + 1, cols] for c in range(3)]
    rows += [ordered[0:1, :TILE], ordered[0:1, TILE:] + offsets]
    for piece in range(PACK // 4):
        part = jnp.concatenate(rows[piece * 4 : piece * 4 + 4], axis=0)
        for peer in range(pack_out.shape[0]):
            pack_out[peer, piece] = part
    local = [row for field in nodes for row in lane_rows(field)]
    local += lane_rows(parent[...].astype(jnp.float32))
    local += [jnp.zeros((1, TILE), jnp.float32)] * (local_out.shape[0] * 4 - len(local))
    for piece in range(len(local) // 4):
        local_out[piece] = jnp.concatenate(local[piece * 4 : piece * 4 + 4], axis=0)


def gather_kernel(
    where_ref,
    held_ref,
    out_ref,
    sources,
    dense,
    receivers,
    totals,
    table_vmem,
    table,
    sems,
    *,
    sizes,
    node_count,
    leaf_count,
):
    shard_z, shard_y, shard_c = sizes
    shards = shard_z * shard_y * shard_c
    tiles = 2 * shards
    per_c = shard_y * shard_z
    per_peer = node_count // shards
    chunks = node_count // TILE
    block = held_ref.shape[0] // shard_c
    local = per_c * PACK
    here = where_ref[0]
    core = here & (shard_c - 1)

    def tile_of(shard):
        low = shard * per_peer // TILE
        high = (shard * per_peer + per_peer - 1) // TILE
        split = jnp.where(high > low, high * TILE - shard * per_peer, per_peer)
        late = split * 2 < per_peer
        return jnp.where(late, high, low), split, late

    tile, split, late = tile_of(here)
    partner = here ^ 1
    _, partner_split, partner_late = tile_of(partner)
    helps = partner_split < per_peer
    helped = jnp.where(partner_late, 0, partner_split)
    helped_count = jnp.where(partner_late, partner_split, per_peer - partner_split)

    column = lax.broadcasted_iota(jnp.int32, (shard_z, TILE), 1)
    beyond = tiles * SOURCE

    def source_tile(entry):
        tile = entry - 1
        owner = tile >> 1
        arrival = (
            (owner & (shard_c - 1)) * per_c
            + ((owner >> (shard_c.bit_length() - 1)) & (shard_y - 1)) * shard_z
            + (owner >> ((shard_c * shard_y).bit_length() - 1))
        )
        return jnp.where(entry == 0, beyond, (arrival * 2 + (tile & 1)) * SOURCE)

    def read(rows, at):
        return jnp.sum(jnp.where(column == at, rows, 0), axis=1, keepdims=True) * QUAD

    for c in range(shard_c):
        for y in range(shard_y):
            begin = c * block + y * shard_z * PACK + 2 * FIELDS
            low = held_ref[pl.ds(begin, shard_z, stride=PACK), :].astype(jnp.int32)
            high = held_ref[pl.ds(begin + 1, shard_z, stride=PACK), :].astype(jnp.int32)
            start = read(high, OFFSETS - TILE + tile)
            stop = read(high, OFFSETS - TILE + tile + 1)
            empty = start == stop
            start = jnp.where(empty, EMPTY * QUAD, start)
            stop = jnp.where(empty, EMPTY * QUAD + QUAD, stop)
            rest = jnp.where(column < OFFSETS - TILE, source_tile(high), 0)
            rest = jnp.where(column == START - TILE, start, rest)
            rest = jnp.where(column == STOP - TILE, stop, rest)
            rows = pl.ds(y * shard_c + c, shard_z, stride=shard_y * shard_c)
            table_vmem[0, rows, :] = source_tile(low)
            table_vmem[1, rows, :] = rest
    extra = lax.broadcasted_iota(jnp.int32, (8, TILE), 1)
    table_vmem[0, shards : shards + 8, :] = jnp.full((8, TILE), beyond, jnp.int32)
    last = jnp.where(extra == START - TILE, EMPTY * QUAD, beyond)
    last = jnp.where(extra == STOP - TILE, EMPTY * QUAD + QUAD, last)
    table_vmem[1, shards : shards + 8, :] = last
    fetches = [
        pltpu.make_async_copy(
            table_vmem.at[half, pl.ds(at, size), :],
            table.at[pl.ds(at, size), pl.ds(half * TILE, TILE)],
            sems.at[n, half],
        )
        for n, (at, size) in enumerate(((0, HEAD), (HEAD, shards + 8 - HEAD)))
        for half in range(2)
    ]
    for fetch in fetches:
        fetch.start()

    for c in range(shard_c):
        for half in range(2):
            base = c * block + half * FIELDS
            rows = [held_ref[pl.ds(base + f, per_c, stride=PACK), :] for f in range(FIELDS)]
            length = jnp.sqrt(rows[3] * rows[3] + rows[4] * rows[4] + rows[5] * rows[5])
            rows += [length * math.pi, length]
            for f, row in enumerate(rows):
                at = c * per_c * 2 * SOURCE + half * SOURCE + f
                sources[pl.ds(at, per_c, stride=2 * SOURCE), :] = row
    blank = lax.broadcasted_iota(jnp.int32, (SOURCE, TILE), 0) >= FIELDS
    sources[tiles * SOURCE : (tiles + 1) * SOURCE, :] = blank.astype(jnp.float32)

    def spread(owner):
        for chunk in range(chunks):
            turned = held_ref[pl.ds(owner * block + local + chunk, 8, stride=chunks), :].T
            for field in range(6):
                dense[field, 8 + chunk * TILE : 8 + (chunk + 1) * TILE, :] = jnp.broadcast_to(
                    turned[:, field : field + 1], (TILE, TILE)
                )

    for field in range(6):
        dense[field, 0:8, :] = jnp.zeros((8, TILE), jnp.float32)
        dense[field, 8 + node_count : 16 + node_count, :] = jnp.zeros((8, TILE), jnp.float32)
        receivers[field, shards * 8 : (shards + 8) * 8, :] = jnp.zeros((64, TILE), jnp.float32)
    spread(core)

    def settle(link, carry):
        for field in range(6):
            receivers[field, pl.ds(pl.multiple_of(link * 8, 8), 8), :] = dense[
                field, pl.ds(8 + link * per_peer, 8), :
            ]
        return carry

    lax.fori_loop(0, shards, settle, 0, unroll=8)

    @pl.when(helps)
    def _():
        spread(1 - core)
        keep = lax.broadcasted_iota(jnp.int32, (8, TILE), 0) < per_peer

        def join(link, carry):
            for field in range(6):
                rows = pl.ds(pl.multiple_of(link * 8, 8), 8)
                theirs = dense[field, pl.ds(8 + link * per_peer + helped - per_peer, 8), :]
                receivers[field, rows, :] = jnp.where(keep, receivers[field, rows, :], theirs)
            return carry

        lax.fori_loop(0, shards, join, 0, unroll=4)

    def one_quad(state):
        shard, spot, end, keep, acc = state
        at = pl.ds(pl.multiple_of(shard * 8, 8), 8)
        rec = [receivers[field, at, :] for field in range(6)]
        acc = [a * keep for a in acc]
        for u in range(QUAD):
            row = pl.multiple_of(table[shard, spot + u], SOURCE)
            src = [sources[pl.ds(row + f, 1), :] for f in range(FIELDS + 2)]
            d = [src[a] - rec[a] for a in range(3)]
            r2 = d[0] * d[0] + d[1] * d[1] + d[2] * d[2]
            toward = rec[3] * d[0] + rec[4] * d[1] + rec[5] * d[2]
            back = src[3] * d[0] + src[4] * d[1] + src[5] * d[2]
            top = jnp.maximum(toward, 0.0) * jnp.maximum(back, 0.0)
            factor = top / ((r2 + src[9]) * (r2 + src[10]))
            acc = [acc[c] + factor * src[6 + c] for c in range(3)]
        for c in range(3):
            totals[c, at, :] = acc[c]
        spot = spot + QUAD
        done = spot >= end
        spot = jnp.where(done, table[shard + 1, START], spot)
        end = jnp.where(done, table[shard + 1, STOP], end)
        shard = jnp.where(done, shard + 1, shard)
        keep = jnp.where(done, 0.0, 1.0)
        return shard, spot, end, keep, acc

    def step(state):
        for _ in range(STEP):
            state = one_quad(state)
        return state

    for fetch in fetches[:2]:
        fetch.wait()
    zero = jnp.zeros((8, TILE), jnp.float32)
    state = (jnp.int32(0), table[0, START], table[0, STOP], jnp.float32(0.0), [zero] * 3)
    state = lax.while_loop(lambda s: s[0] < HEAD - STEP, step, state)
    for fetch in fetches[2:]:
        fetch.wait()
    lax.while_loop(lambda s: s[0] < shards, step, state)

    places = shards * 8
    ones = jnp.ones((8, TILE), jnp.float32)
    parts = []
    for c in range(3):
        left = lax.dot_general(
            ones,
            totals[c, 0:places, :],
            NT_DIMS,
            precision=EXACT,
            preferred_element_type=jnp.float32,
        )[0:1, :]
        for _ in range(3):
            near = left.astype(jnp.bfloat16)
            parts.append(near.astype(jnp.float32))
            left = left - parts[-1]
    parts = jnp.concatenate(parts + [jnp.zeros((7, places), jnp.float32)], axis=0)
    parts = parts.astype(jnp.bfloat16)
    place = lax.broadcasted_iota(jnp.int32, (places, TILE), 0)
    lane = lax.broadcasted_iota(jnp.int32, (places, TILE), 1)
    link = place >> 3
    slot = place & 7

    def collect(owner, node):
        pieces = []
        for chunk in range(leaf_count // TILE):
            row = owner * block + local + 6 * chunks + chunk
            parent = held_ref[pl.ds(row, 1), :].astype(jnp.int32) + leaf_count
            leaf = lane + chunk * TILE
            picked = jnp.where(node == leaf, 1.0, 0.0) + jnp.where(node == parent, 1.0, 0.0)
            sums = jnp.dot(
                parts, picked.astype(jnp.bfloat16), preferred_element_type=jnp.float32
            )
            pieces.append(
                jnp.concatenate(
                    [sums[3 * c : 3 * c + 1] + sums[3 * c + 1 : 3 * c + 2] + sums[3 * c + 2 : 3 * c + 3] for c in range(3)],
                    axis=0,
                )
            )
        return jnp.concatenate(pieces, axis=1)

    first_slot = jnp.where(late, split, 0)
    last_slot = jnp.where(late, per_peer, split)
    mine = (slot >= first_slot) & (slot < last_slot)
    result = collect(core, jnp.where(mine, link * per_peer + slot, -1))
    groups = out_ref.shape[0] // shard_c
    for group in range(groups):
        out_ref[group * shard_c + core] = result

    @pl.when(helps)
    def _():
        theirs = (slot >= per_peer) & (slot < per_peer + helped_count)
        node = jnp.where(theirs, link * per_peer + helped + slot - per_peer, -1)
        result = collect(1 - core, node)
        for group in range(groups):
            out_ref[group * shard_c + 1 - core] = result

    @pl.when(jnp.logical_not(helps))
    def _():
        for group in range(groups):
            out_ref[group * shard_c + 1 - core] = jnp.zeros((3, leaf_count), jnp.float32)


def gather_call(where, everything, sizes, groups, node_count, leaf_count):
    shards = sizes[0] * sizes[1] * sizes[2]
    return pl.pallas_call(
        functools.partial(
            gather_kernel, sizes=sizes, node_count=node_count, leaf_count=leaf_count
        ),
        out_shape=jax.ShapeDtypeStruct((groups * sizes[2], 3, leaf_count), jnp.float32),
        in_specs=[
            pl.BlockSpec(memory_space=pltpu.SMEM),
            pl.BlockSpec(memory_space=pltpu.VMEM),
        ],
        out_specs=pl.BlockSpec(memory_space=pltpu.VMEM),
        scratch_shapes=[
            pltpu.VMEM(((2 * shards + 1) * SOURCE, TILE), jnp.float32),
            pltpu.VMEM((6, node_count + 16, TILE), jnp.float32),
            pltpu.VMEM((6, (shards + 8) * 8, TILE), jnp.float32),
            pltpu.VMEM((3, (shards + 8) * 8, TILE), jnp.float32),
            pltpu.VMEM((2, shards + 8, TILE), jnp.int32),
            pltpu.SMEM((shards + 8, 2 * TILE), jnp.int32),
            pltpu.SemaphoreType.DMA((2, 2)),
        ],
        compiler_params=pltpu.CompilerParams(vmem_limit_bytes=40 * 1024 * 1024),
        name="gather",
    )(where, everything)


def body(
    leaf_emit,
    leaf_albedo,
    leaf_radiosity,
    leaf_area,
    parent_index,
    node_position,
    node_angles,
    block_receiver,
    block_source,
    block_count,
):
    leaf_count = leaf_area.shape[0]
    node_count = node_position.shape[1]
    sizes = tuple(lax.axis_size(axis) for axis in DEV)
    groups = lax.axis_size("grp")
    vmem = pl.BlockSpec(memory_space=pltpu.VMEM)
    own_rows = 8 * node_count // TILE
    held, local = pl.pallas_call(
        pack_kernel,
        out_shape=(
            jax.ShapeDtypeStruct((sizes[0], PACK // 4, 4, TILE), jnp.float32),
            jax.ShapeDtypeStruct((own_rows // 4, 4, TILE), jnp.float32),
        ),
        in_specs=[vmem] * 8,
        out_specs=(vmem, vmem),
        name="pack",
    )(
        leaf_radiosity,
        leaf_area[None, :],
        parent_index[None, :],
        node_position,
        node_angles,
        block_receiver,
        block_source,
        block_count,
    )
    held = lax.all_to_all(held, DEV[0], 0, 0, tiled=True).reshape(-1, 4, TILE)
    held = lax.all_to_all(
        jnp.broadcast_to(held[None], (sizes[1], *held.shape)), DEV[1], 0, 0, tiled=True
    )
    held = jnp.concatenate([held.reshape(-1, 4, TILE), local], axis=0)
    held = lax.all_to_all(
        jnp.broadcast_to(held[None], (sizes[2], *held.shape)), DEV[2], 0, 0, tiled=True
    )
    where = lax.axis_index(DEV).astype(jnp.int32).reshape(1)
    partial = gather_call(where, held.reshape(-1, TILE), sizes, groups, node_count, leaf_count)
    gathered = lax.all_to_all(partial, ("grp", DEV[2]), 0, 0, tiled=True).sum(axis=0)
    return leaf_emit + leaf_albedo * gathered


def solution(mesh):
    split = Mesh(
        mesh.devices.reshape(mesh.shape["grp"], 16, 4, 2), ("grp", "dev_0", "dev_1", "dev_2")
    )
    placed = (
        P(None, DEV),
        P(None, DEV),
        P(None, DEV),
        P(DEV),
        P(DEV),
        P(None, DEV),
        P(None, DEV),
        P("grp", DEV),
        P("grp", DEV),
        P("grp", DEV),
    )
    return jax.shard_map(body, mesh=split, in_specs=placed, out_specs=P(None, DEV), check_vma=False)
```

time: 90.2 us -> 78.1 us (0.87)
  the two profiles are of different devices: /device:TPU:81 before, /device:TPU:1 now
where the time goes in v2:
time: 78.1 us; the launch traced here: 77.7 us
  blocking collectives  47.2 us (60%)
  Pallas kernels  16.1 us (21%)
  waiting for transfers between devices  7.64 us (10%)
  starting transfers between devices  4.18 us (5%)
  local copies, waits for them, and re-layouts  1.11 us (1%)
    all_to_all x1, blocking collectives, body(): held = lax.all_to_all(held, DEV[0], 0, 0, tiled=True).reshape(-1, 4, TILE)  28.1 us
    pallas_call x1, Pallas kernels, gather_call(): pl.pallas_call(functools.partial(gather_kernel, sizes=sizes, node_count=n...  13.9 us
    all_to_all x1, blocking collectives, body(): lax.all_to_all(jnp.broadcast_to(held[None], (sizes[2], *held.shape)), DEV...  10.2 us
    all_to_all x1, blocking collectives, body(): lax.all_to_all(partial, ('grp', DEV[2]), 0, 0, tiled=True).sum(axis=0)  8.84 us
    all_to_all x1, waiting for transfers between devices, body(): lax.all_to_all(jnp.broadcast_to(held[None], (sizes[1], *held.shape)), DEV...  7.64 us
    all_to_all x1, starting transfers between devices, body(): lax.all_to_all(jnp.broadcast_to(held[None], (sizes[1], *held.shape)), DEV...  4.18 us
    pallas_call x1, Pallas kernels, body(): pl.pallas_call(pack_kernel, out_shape=(jax.ShapeDtypeStruct((sizes[0], PA...  2.19 us
  transfers between devices with their start and end apart: 1, of which 1 were waited for; matrix products, arithmetic and copies ran while one was open for 0% of the time, Pallas kernels for 0%

profile of v2, /device:TPU:1, one launch (start us, length us, event | category | flops | bytes accessed | tf_op | source)
XLA Modules:
  0.0 77.7 jit_solution(12673692082652454803)
XLA Ops:
  0.7 2.2 %pack.1 = (f32[16,5,4,128]{3,2,1,0:T(4,128)}, f32[12,4,128]{2,1,0:T(4,128)}) custom-call(f32[3,512]{1,0:T(4,128)} %radiosity.1, f32[1,512]{1,0:T(1,128)} %bitcast.9, s32[1,512]{1,0:T(1,128)} %bitcast.10, f32[3,768]{1,0:T(4,128)} %position.1, f32[2,768]{1,0:T(2,128)} %angles.1, s32[1,128]{1,0:T(1,128)} %receiver.1, s32[1,128]{1,0:T(1,128)} %source.1, ...), custom_call_target="tpu_custom_call" | custom-call | tf_op jit(solution)/shard_map/pack/pallas_call | solution.py:382
  2.8 0.0 copy-start
  2.8 28.1 %all_to_all.20 = f32[16,5,4,128]{3,2,1,0:T(4,128)S(1)} all-to-all(f32[16,5,4,128]{3,2,1,0:T(4,128)} %get-tuple-element.7), channel_id=1, replica_groups=mesh['grp'=4,'dev_0'=16,'dev_1'=4,'dev_2'=2] {'dev_0'}, dimensions={0} | all-to-all | bytes 327680 | tf_op jit(solution)/shard_map/all_to_all | solution.py:401
  30.9 0.9 %broadcast_in_dim.22 = f32[4,80,4,128]{3,2,1,0:T(4,128)} broadcast(f32[80,4,128]{2,1,0:T(4,128)S(1)} %bitcast.8), dimensions={1,2,3} | broadcast | bytes 819200 | tf_op jit(solution)/shard_map/broadcast_in_dim | solution.py:403
  31.9 4.2 %all-to-all-start.1 = ((f32[4,80,4,128]{3,2,1,0:T(4,128)}), f32[4,80,4,128]{3,2,1,0:T(4,128)S(1)}, u32[]{:S(2)}, u32[]{:S(2)}) async-start(f32[4,80,4,128]{3,2,1,0:T(4,128)} %broadcast_in_dim.22), calls=%async_computation.1 | async-start | bytes 1310720 | tf_op jit(solution)/shard_map/all_to_all | solution.py:402
  36.0 7.6 %all-to-all-done.1 = f32[4,80,4,128]{3,2,1,0:T(4,128)S(1)} async-done(((f32[4,80,4,128]{3,2,1,0:T(4,128)}), f32[4,80,4,128]{3,2,1,0:T(4,128)S(1)}, u32[]{:S(2)}, u32[]{:S(2)}) %all-to-all-start.1) | async-done | bytes 655392 | tf_op jit(solution)/shard_map/all_to_all | solution.py:402
  43.7 0.0 copy-done
  43.7 0.1 pad_maximum_fusion
  43.8 0.2 broadcast_in_dim.23
  44.0 10.2 %all_to_all.21 = f32[2,332,4,128]{3,2,1,0:T(4,128)S(1)} all-to-all(f32[2,332,4,128]{3,2,1,0:T(4,128)S(1)} %broadcast_in_dim.23), channel_id=1, replica_groups=mesh['grp'=4,'dev_0'=16,'dev_1'=4,'dev_2'=2] {'dev_2'}, dimensions={0} | all-to-all | bytes 2719744 | tf_op jit(solution)/shard_map/all_to_all | solution.py:406
  54.3 0.0 copy-start.1
  54.3 0.0 copy-start.2
  54.3 13.9 %gather.1 = f32[8,3,512]{2,1,0:T(4,128)S(1)} custom-call(s32[1]{0:T(128)} %bitcast.where_ref, f32[2656,128]{1,0:T(8,128)S(1)} %bitcast.6), custom_call_target="tpu_custom_call" | custom-call | tf_op jit(solution)/shard_map/gather/pallas_call | solution.py:340
  68.2 8.8 %all_to_all.22 = f32[8,3,512]{2,1,0:T(4,128)S(1)} all-to-all(f32[8,3,512]{2,1,0:T(4,128)S(1)} %gather.1), channel_id=1, replica_groups=mesh['grp'=4,'dev_0'=16,'dev_1'=4,'dev_2'=2] {'grp','dev_2'}, dimensions={0} | all-to-all | bytes 98304 | tf_op jit(solution)/shard_map/all_to_all | solution.py:411
  77.1 0.0 copy-done.1
  77.1 0.0 copy-done.2
  77.1 0.6 multiply_add_fusion
  (1 shorter events, 0.0 us)
Async XLA Ops:
  2.8 40.8 %copy-start = (f32[12,4,128]{2,1,0:T(4,128)S(1)}, f32[12,4,128]{2,1,0:T(4,128)}, u32[]{:S(2)}) copy-start(f32[12,4,128]{2,1,0:T(4,128)} %get-tuple-element.8) | copy-start | bytes 73732
  31.9 11.8 %all-to-all-start.1 = ((f32[4,80,4,128]{3,2,1,0:T(4,128)}), f32[4,80,4,128]{3,2,1,0:T(4,128)S(1)}, u32[]{:S(2)}, u32[]{:S(2)}) async-start(f32[4,80,4,128]{3,2,1,0:T(4,128)} %broadcast_in_dim.22), calls=%async_computation.1 | async-start | bytes 1310720 | tf_op jit(solution)/shard_map/all_to_all | solution.py:402
  54.3 22.8 %copy-start.1 = (f32[3,512]{1,0:T(4,128)S(1)}, f32[3,512]{1,0:T(4,128)}, u32[]{:S(2)}) copy-start(f32[3,512]{1,0:T(4,128)} %param.10) | copy-start | bytes 18436
  54.3 22.8 %copy-start.2 = (f32[3,512]{1,0:T(4,128)S(1)}, f32[3,512]{1,0:T(4,128)}, u32[]{:S(2)}) copy-start(f32[3,512]{1,0:T(4,128)} %param.11) | copy-start | bytes 18436

commit v3 on v2

--- a/solution.py
+++ b/solution.py
@@ -12,15 +12,14 @@
 TILE = 128
 DEV = ("dev_0", "dev_1", "dev_2")
 QUAD = 4
+QUADS = 40
 STEP = 4
 PACK = 20
 FIELDS = 9
 SOURCE = 16
 OFFSETS = 248
-EMPTY = 40
-START = 254
-STOP = 255
-HEAD = 32
+SHIFT = 1 << 13
+CHUNK = 512
 EXACT = lax.Precision.HIGHEST
 NT_DIMS = (((1,), (1,)), ((), ()))
 
@@ -67,7 +66,9 @@
     first = jnp.zeros((8, slots), jnp.float32)
     for t in range(7):
         first = first + jnp.where(tiles > t, quads[t : t + 1, :], 0.0)
-    spot = jnp.sum(member * (first * QUAD + place), axis=0, keepdims=True)
+    quad = jnp.floor(place * (1.0 / QUAD))
+    turn = place - quad * QUAD
+    spot = jnp.sum(member * (first + quad + turn * QUADS), axis=0, keepdims=True)
     alive = jnp.sum(member, axis=0, keepdims=True)
     spot = jnp.where(alive > 0.0, spot, -1.0).astype(jnp.int32)
     to_spot = (lax.broadcasted_iota(jnp.int32, (2 * slots, slots), 0) == spot).astype(jnp.float32)
@@ -97,15 +98,20 @@
 
 def gather_kernel(
     where_ref,
-    held_ref,
+    own_ref,
+    other_ref,
+    emit_ref,
+    albedo_ref,
     out_ref,
+    emit_out,
+    albedo_out,
     sources,
     dense,
     receivers,
     totals,
     table_vmem,
     table,
-    sems,
+    sem,
     *,
     sizes,
     node_count,
@@ -117,7 +123,9 @@
     per_c = shard_y * shard_z
     per_peer = node_count // shards
     chunks = node_count // TILE
-    block = held_ref.shape[0] // shard_c
+    blocks = (own_ref, other_ref)
+    emit_out[...] = emit_ref[...]
+    albedo_out[...] = albedo_ref[...]
     local = per_c * PACK
     here = where_ref[0]
     core = here & (shard_c - 1)
@@ -136,59 +144,90 @@
     helped = jnp.where(partner_late, 0, partner_split)
     helped_count = jnp.where(partner_late, partner_split, per_peer - partner_split)
 
-    column = lax.broadcasted_iota(jnp.int32, (shard_z, TILE), 1)
-    beyond = tiles * SOURCE
-
-    def source_tile(entry):
-        tile = entry - 1
-        owner = tile >> 1
-        arrival = (
-            (owner & (shard_c - 1)) * per_c
-            + ((owner >> (shard_c.bit_length() - 1)) & (shard_y - 1)) * shard_z
-            + (owner >> ((shard_c * shard_y).bit_length() - 1))
+    def list_rows(at):
+        return jnp.concatenate(
+            [ref[pl.ds(at, per_c, stride=PACK), :] for ref in blocks], axis=0
         )
-        return jnp.where(entry == 0, beyond, (arrival * 2 + (tile & 1)) * SOURCE)
-
-    def read(rows, at):
-        return jnp.sum(jnp.where(column == at, rows, 0), axis=1, keepdims=True) * QUAD
-
-    for c in range(shard_c):
-        for y in range(shard_y):
-            begin = c * block + y * shard_z * PACK + 2 * FIELDS
-            low = held_ref[pl.ds(begin, shard_z, stride=PACK), :].astype(jnp.int32)
-            high = held_ref[pl.ds(begin + 1, shard_z, stride=PACK), :].astype(jnp.int32)
-            start = read(high, OFFSETS - TILE + tile)
-            stop = read(high, OFFSETS - TILE + tile + 1)
-            empty = start == stop
-            start = jnp.where(empty, EMPTY * QUAD, start)
-            stop = jnp.where(empty, EMPTY * QUAD + QUAD, stop)
-            rest = jnp.where(column < OFFSETS - TILE, source_tile(high), 0)
-            rest = jnp.where(column == START - TILE, start, rest)
-            rest = jnp.where(column == STOP - TILE, stop, rest)
-            rows = pl.ds(y * shard_c + c, shard_z, stride=shard_y * shard_c)
-            table_vmem[0, rows, :] = source_tile(low)
-            table_vmem[1, rows, :] = rest
-    extra = lax.broadcasted_iota(jnp.int32, (8, TILE), 1)
-    table_vmem[0, shards : shards + 8, :] = jnp.full((8, TILE), beyond, jnp.int32)
-    last = jnp.where(extra == START - TILE, EMPTY * QUAD, beyond)
-    last = jnp.where(extra == STOP - TILE, EMPTY * QUAD + QUAD, last)
-    table_vmem[1, shards : shards + 8, :] = last
-    fetches = [
-        pltpu.make_async_copy(
-            table_vmem.at[half, pl.ds(at, size), :],
-            table.at[pl.ds(at, size), pl.ds(half * TILE, TILE)],
-            sems.at[n, half],
+
+    low = list_rows(2 * FIELDS)
+    high = list_rows(2 * FIELDS + 1)
+    lane = lax.broadcasted_iota(jnp.int32, (shards, TILE), 1)
+    arrival = lax.broadcasted_iota(jnp.int32, (shards, TILE), 0)
+    first = jnp.sum(jnp.where(lane == OFFSETS - TILE + tile, high, 0.0), axis=1, keepdims=True)
+    last = jnp.sum(jnp.where(lane == OFFSETS - TILE + tile + 1, high, 0.0), axis=1, keepdims=True)
+    count = jnp.broadcast_to(last - first, (shards, TILE))
+    upto = jnp.dot(
+        (lane <= arrival).astype(jnp.bfloat16),
+        count.astype(jnp.bfloat16),
+        preferred_element_type=jnp.float32,
+    )
+    ahead = upto - count
+    shift = first - ahead + SHIFT
+    coarse = jnp.floor(shift * (1.0 / TILE))
+    high = jnp.where(lane < OFFSETS - TILE, high, 0.0)
+    extras = (arrival.astype(jnp.float32), coarse, shift - coarse * TILE, first)
+    for n, extra in enumerate(extras):
+        high = jnp.where(lane == OFFSETS - TILE + n, extra, high)
+    listed = jnp.concatenate([low, high], axis=1).astype(jnp.bfloat16)
+
+    def lay_out(chunk):
+        spot = lax.broadcasted_iota(jnp.int32, (1, CHUNK), 1) + chunk * CHUNK
+        place = spot.astype(jnp.float32)
+        chosen = jnp.concatenate(
+            [
+                jnp.where((ahead <= part) & (part < upto), 1.0, 0.0)
+                for part in lane_rows(place)
+            ],
+            axis=1,
+        ).astype(jnp.bfloat16)
+        found = lax.dot_general(
+            listed, chosen, (((0,), (0,)), ((), ())), preferred_element_type=jnp.float32
         )
-        for n, (at, size) in enumerate(((0, HEAD), (HEAD, shards + 8 - HEAD)))
-        for half in range(2)
-    ]
-    for fetch in fetches:
-        fetch.start()
-
-    for c in range(shard_c):
+        owner = found[OFFSETS : OFFSETS + 1, :].astype(jnp.int32)
+        quad = found[OFFSETS + 1 : OFFSETS + 2, :] * TILE + found[OFFSETS + 2 : OFFSETS + 3, :]
+        quad = quad - SHIFT + place
+        goes_on = jnp.where(quad > found[OFFSETS + 3 : OFFSETS + 4, :], 1, 0)
+        quads = lax.broadcasted_iota(jnp.int32, (QUADS, CHUNK), 0).astype(jnp.float32)
+        match = quads == quad
+        entries = jnp.concatenate(
+            [
+                jnp.sum(
+                    jnp.where(match, found[u * QUADS : (u + 1) * QUADS, :], 0.0),
+                    axis=0,
+                    keepdims=True,
+                )
+                for u in range(QUAD)
+            ],
+            axis=0,
+        ).astype(jnp.int32)
+        source = entries - 1
+        giver = source >> 1
+        came = (
+            ((giver & (shard_c - 1)) ^ core) * per_c
+            + ((giver >> (shard_c.bit_length() - 1)) & (shard_y - 1)) * shard_z
+            + (giver >> ((shard_c * shard_y).bit_length() - 1))
+        )
+        rows = jnp.where(entries == 0, tiles, came * 2 + (source & 1)) * SOURCE
+        link = (
+            (owner & (shard_z - 1)) * (shard_y * shard_c)
+            + ((owner >> (shard_z.bit_length() - 1)) & (shard_y - 1)) * shard_c
+            + ((owner >> (per_c.bit_length() - 1)) ^ core)
+        )
+        total = jnp.concatenate([upto[shards - 1 : shards, :]] * (CHUNK // TILE), axis=1)
+        total = total.astype(jnp.int32)
+        link = jnp.where(spot < total, link, shards) * 8
+        table_vmem[...] = jnp.concatenate(
+            [rows, link, goes_on, total, jnp.zeros((1, CHUNK), jnp.int32)], axis=0
+        )
+        return pltpu.make_async_copy(table_vmem, table, sem)
+
+    fetch = lay_out(0)
+    fetch.start()
+
+    for c, ref in enumerate(blocks):
         for half in range(2):
-            base = c * block + half * FIELDS
-            rows = [held_ref[pl.ds(base + f, per_c, stride=PACK), :] for f in range(FIELDS)]
+            base = half * FIELDS
+            rows = [ref[pl.ds(base + f, per_c, stride=PACK), :] for f in range(FIELDS)]
             length = jnp.sqrt(rows[3] * rows[3] + rows[4] * rows[4] + rows[5] * rows[5])
             rows += [length * math.pi, length]
             for f, row in enumerate(rows):
@@ -197,9 +236,9 @@
     blank = lax.broadcasted_iota(jnp.int32, (SOURCE, TILE), 0) >= FIELDS
     sources[tiles * SOURCE : (tiles + 1) * SOURCE, :] = blank.astype(jnp.float32)
 
-    def spread(owner):
+    def spread(ref):
         for chunk in range(chunks):
-            turned = held_ref[pl.ds(owner * block + local + chunk, 8, stride=chunks), :].T
+            turned = ref[pl.ds(local + chunk, 8, stride=chunks), :].T
             for field in range(6):
                 dense[field, 8 + chunk * TILE : 8 + (chunk + 1) * TILE, :] = jnp.broadcast_to(
                     turned[:, field : field + 1], (TILE, TILE)
@@ -209,7 +248,7 @@
         dense[field, 0:8, :] = jnp.zeros((8, TILE), jnp.float32)
         dense[field, 8 + node_count : 16 + node_count, :] = jnp.zeros((8, TILE), jnp.float32)
         receivers[field, shards * 8 : (shards + 8) * 8, :] = jnp.zeros((64, TILE), jnp.float32)
-    spread(core)
+    spread(own_ref)
 
     def settle(link, carry):
         for field in range(6):
@@ -222,7 +261,7 @@
 
     @pl.when(helps)
     def _():
-        spread(1 - core)
+        spread(other_ref)
         keep = lax.broadcasted_iota(jnp.int32, (8, TILE), 0) < per_peer
 
         def join(link, carry):
@@ -234,44 +273,44 @@
 
         lax.fori_loop(0, shards, join, 0, unroll=4)
 
-    def one_quad(state):
-        shard, spot, end, keep, acc = state
-        at = pl.ds(pl.multiple_of(shard * 8, 8), 8)
-        rec = [receivers[field, at, :] for field in range(6)]
-        acc = [a * keep for a in acc]
-        for u in range(QUAD):
-            row = pl.multiple_of(table[shard, spot + u], SOURCE)
-            src = [sources[pl.ds(row + f, 1), :] for f in range(FIELDS + 2)]
-            d = [src[a] - rec[a] for a in range(3)]
-            r2 = d[0] * d[0] + d[1] * d[1] + d[2] * d[2]
-            toward = rec[3] * d[0] + rec[4] * d[1] + rec[5] * d[2]
-            back = src[3] * d[0] + src[4] * d[1] + src[5] * d[2]
-            top = jnp.maximum(toward, 0.0) * jnp.maximum(back, 0.0)
-            factor = top / ((r2 + src[9]) * (r2 + src[10]))
-            acc = [acc[c] + factor * src[6 + c] for c in range(3)]
-        for c in range(3):
-            totals[c, at, :] = acc[c]
-        spot = spot + QUAD
-        done = spot >= end
-        spot = jnp.where(done, table[shard + 1, START], spot)
-        end = jnp.where(done, table[shard + 1, STOP], end)
-        shard = jnp.where(done, shard + 1, shard)
-        keep = jnp.where(done, 0.0, 1.0)
-        return shard, spot, end, keep, acc
-
-    def step(state):
-        for _ in range(STEP):
-            state = one_quad(state)
-        return state
-
-    for fetch in fetches[:2]:
-        fetch.wait()
+    for c in range(3):
+        totals[c, :, :] = jnp.zeros(((shards + 8) * 8, TILE), jnp.float32)
+
+    def step(turn, acc):
+        for n in range(STEP):
+            spot = turn * STEP + n
+            at = pl.ds(pl.multiple_of(table[QUAD, spot], 8), 8)
+            keep = jnp.where(table[QUAD + 1, spot] > 0, 1.0, 0.0)
+            rec = [receivers[field, at, :] for field in range(6)]
+            acc = [a * keep for a in acc]
+            for u in range(QUAD):
+                row = pl.multiple_of(table[u, spot], SOURCE)
+                src = [sources[pl.ds(row + f, 1), :] for f in range(FIELDS + 2)]
+                d = [src[a] - rec[a] for a in range(3)]
+                r2 = d[0] * d[0] + d[1] * d[1] + d[2] * d[2]
+                toward = rec[3] * d[0] + rec[4] * d[1] + rec[5] * d[2]
+                back = src[3] * d[0] + src[4] * d[1] + src[5] * d[2]
+                top = jnp.maximum(toward, 0.0) * jnp.maximum(back, 0.0)
+                factor = top / ((r2 + src[9]) * (r2 + src[10]))
+                acc = [acc[c] + factor * src[6 + c] for c in range(3)]
+            for c in range(3):
+                totals[c, at, :] = acc[c]
+        return acc
+
+    def work_off(chunk, acc):
+        held = jnp.clip(table[QUAD + 2, 0] - chunk * CHUNK, 0, CHUNK)
+        return lax.fori_loop(0, (held + STEP - 1) // STEP, step, acc)
+
+    def next_chunk(chunk, acc):
+        again = lay_out(chunk)
+        again.start()
+        again.wait()
+        return work_off(chunk, acc)
+
     zero = jnp.zeros((8, TILE), jnp.float32)
-    state = (jnp.int32(0), table[0, START], table[0, STOP], jnp.float32(0.0), [zero] * 3)
-    state = lax.while_loop(lambda s: s[0] < HEAD - STEP, step, state)
-    for fetch in fetches[2:]:
-        fetch.wait()
-    lax.while_loop(lambda s: s[0] < shards, step, state)
+    fetch.wait()
+    acc = work_off(0, [zero] * 3)
+    lax.fori_loop(1, (table[QUAD + 2, 0] + CHUNK - 1) // CHUNK, next_chunk, acc)
 
     places = shards * 8
     ones = jnp.ones((8, TILE), jnp.float32)
@@ -295,11 +334,10 @@
     link = place >> 3
     slot = place & 7
 
-    def collect(owner, node):
+    def collect(ref, node):
         pieces = []
         for chunk in range(leaf_count // TILE):
-            row = owner * block + local + 6 * chunks + chunk
-            parent = held_ref[pl.ds(row, 1), :].astype(jnp.int32) + leaf_count
+            parent = ref[pl.ds(local + 6 * chunks + chunk, 1), :].astype(jnp.int32) + leaf_count
             leaf = lane + chunk * TILE
             picked = jnp.where(node == leaf, 1.0, 0.0) + jnp.where(node == parent, 1.0, 0.0)
             sums = jnp.dot(
@@ -316,7 +354,7 @@
     first_slot = jnp.where(late, split, 0)
     last_slot = jnp.where(late, per_peer, split)
     mine = (slot >= first_slot) & (slot < last_slot)
-    result = collect(core, jnp.where(mine, link * per_peer + slot, -1))
+    result = collect(own_ref, jnp.where(mine, link * per_peer + slot, -1))
     groups = out_ref.shape[0] // shard_c
     for group in range(groups):
         out_ref[group * shard_c + core] = result
@@ -325,7 +363,7 @@
     def _():
         theirs = (slot >= per_peer) & (slot < per_peer + helped_count)
         node = jnp.where(theirs, link * per_peer + helped + slot - per_peer, -1)
-        result = collect(1 - core, node)
+        result = collect(other_ref, node)
         for group in range(groups):
             out_ref[group * shard_c + 1 - core] = result
 
@@ -335,30 +373,32 @@
             out_ref[group * shard_c + 1 - core] = jnp.zeros((3, leaf_count), jnp.float32)
 
 
-def gather_call(where, everything, sizes, groups, node_count, leaf_count):
+def gather_call(where, own, other, emit, albedo, sizes, groups, node_count, leaf_count):
     shards = sizes[0] * sizes[1] * sizes[2]
     return pl.pallas_call(
         functools.partial(
             gather_kernel, sizes=sizes, node_count=node_count, leaf_count=leaf_count
         ),
-        out_shape=jax.ShapeDtypeStruct((groups * sizes[2], 3, leaf_count), jnp.float32),
-        in_specs=[
-            pl.BlockSpec(memory_space=pltpu.SMEM),
-            pl.BlockSpec(memory_space=pltpu.VMEM),
-        ],
-        out_specs=pl.BlockSpec(memory_space=pltpu.VMEM),
+        out_shape=(
+            jax.ShapeDtypeStruct((groups * sizes[2], 3, leaf_count), jnp.float32),
+            jax.ShapeDtypeStruct(emit.shape, jnp.float32),
+            jax.ShapeDtypeStruct(albedo.shape, jnp.float32),
+        ),
+        in_specs=[pl.BlockSpec(memory_space=pltpu.SMEM)]
+        + [pl.BlockSpec(memory_space=pltpu.VMEM)] * 4,
+        out_specs=(pl.BlockSpec(memory_space=pltpu.VMEM),) * 3,
         scratch_shapes=[
             pltpu.VMEM(((2 * shards + 1) * SOURCE, TILE), jnp.float32),
             pltpu.VMEM((6, node_count + 16, TILE), jnp.float32),
             pltpu.VMEM((6, (shards + 8) * 8, TILE), jnp.float32),
             pltpu.VMEM((3, (shards + 8) * 8, TILE), jnp.float32),
-            pltpu.VMEM((2, shards + 8, TILE), jnp.int32),
-            pltpu.SMEM((shards + 8, 2 * TILE), jnp.int32),
-            pltpu.SemaphoreType.DMA((2, 2)),
+            pltpu.VMEM((8, CHUNK), jnp.int32),
+            pltpu.SMEM((8, CHUNK), jnp.int32),
+            pltpu.SemaphoreType.DMA(()),
         ],
-        compiler_params=pltpu.CompilerParams(vmem_limit_bytes=40 * 1024 * 1024),
+        compiler_params=pltpu.CompilerParams(vmem_limit_bytes=20 * 1024 * 1024),
         name="gather",
-    )(where, everything)
+    )(where, own, other, emit, albedo)
 
 
 def body(
@@ -403,13 +443,21 @@
         jnp.broadcast_to(held[None], (sizes[1], *held.shape)), DEV[1], 0, 0, tiled=True
     )
     held = jnp.concatenate([held.reshape(-1, 4, TILE), local], axis=0)
-    held = lax.all_to_all(
-        jnp.broadcast_to(held[None], (sizes[2], *held.shape)), DEV[2], 0, 0, tiled=True
-    )
+    other = lax.ppermute(held, DEV[2], [(0, 1), (1, 0)])
     where = lax.axis_index(DEV).astype(jnp.int32).reshape(1)
-    partial = gather_call(where, held.reshape(-1, TILE), sizes, groups, node_count, leaf_count)
+    partial, emit, albedo = gather_call(
+        where,
+        held.reshape(-1, TILE),
+        other.reshape(-1, TILE),
+        leaf_emit,
+        leaf_albedo,
+        sizes,
+        groups,
+        node_count,
+        leaf_count,
+    )
     gathered = lax.all_to_all(partial, ("grp", DEV[2]), 0, 0, tiled=True).sum(axis=0)
-    return leaf_emit + leaf_albedo * gathered
+    return emit + albedo * gathered
 
 
 def solution(mesh):

time: 78.1 us -> 75.3 us (0.964)
  waiting for transfers between devices: 7.64 us -> 1.71 us
  starting transfers between devices: 4.18 us -> 7.71 us
  blocking collectives: 47.2 us -> 48.6 us
  local copies, waits for them, and re-layouts: 1.11 us -> 0.1 us
    ppermute x0 -> x1, starting transfers between devices: none -> 7.71 us  [body(): other = lax.ppermute(held, DEV[2], [(0, 1), (1, 0)])]
    all_to_all x1 -> x0, waiting for transfers between devices: 7.64 us -> none  [body(): lax.all_to_all(jnp.broadcast_to(held[None], (sizes[1], *held.shape)), DEV...]
    all_to_all x1 -> x0, starting transfers between devices: 4.18 us -> none  [body(): lax.all_to_all(jnp.broadcast_to(held[None], (sizes[1], *held.shape)), DEV...]
    ppermute x0 -> x1, waiting for transfers between devices: none -> 1.71 us  [body(): other = lax.ppermute(held, DEV[2], [(0, 1), (1, 0)])]
    all_to_all x1, blocking collectives: 10.2 us -> 11.6 us  [body(): lax.all_to_all(jnp.broadcast_to(held[None], (sizes[1], *held.shape)), DEV...]
    broadcast_in_dim x1, local copies, waits for them, and re-layouts: 0.92 us -> 0.09 us  [body(): jnp.broadcast_to(held[None], (sizes[1], *held.shape))]
where the time goes in v3:
time: 75.3 us; the launch traced here: 74.9 us
  blocking collectives  48.6 us (65%)
  Pallas kernels  15.4 us (20%)
  starting transfers between devices  7.71 us (10%)
  waiting for transfers between devices  1.71 us (2%)
  other arithmetic  0.78 us (1%)
    all_to_all x1, blocking collectives, body(): held = lax.all_to_all(held, DEV[0], 0, 0, tiled=True).reshape(-1, 4, TILE)  28 us
    pallas_call x1, Pallas kernels, gather_call(): pl.pallas_call(functools.partial(gather_kernel, sizes=sizes, node_count=n...  13.2 us
    all_to_all x1, blocking collectives, body(): lax.all_to_all(jnp.broadcast_to(held[None], (sizes[1], *held.shape)), DEV...  11.6 us
    all_to_all x1, blocking collectives, body(): lax.all_to_all(partial, ('grp', DEV[2]), 0, 0, tiled=True).sum(axis=0)  8.98 us
    ppermute x1, starting transfers between devices, body(): other = lax.ppermute(held, DEV[2], [(0, 1), (1, 0)])  7.71 us
    pallas_call x1, Pallas kernels, body(): pl.pallas_call(pack_kernel, out_shape=(jax.ShapeDtypeStruct((sizes[0], PA...  2.19 us
    ppermute x1, waiting for transfers between devices, body(): other = lax.ppermute(held, DEV[2], [(0, 1), (1, 0)])  1.71 us
  transfers between devices with their start and end apart: 1, of which 1 were waited for; matrix products, arithmetic and copies ran while one was open for 0% of the time, Pallas kernels for 0%

profile of v3, /device:TPU:1, one launch (start us, length us, event | category | flops | bytes accessed | tf_op | source)
XLA Modules:
  0.0 74.9 jit_solution(12670588523570321253)
XLA Ops:
  0.7 2.2 %pack.1 = (f32[16,5,4,128]{3,2,1,0:T(4,128)}, f32[12,4,128]{2,1,0:T(4,128)}) custom-call(f32[3,512]{1,0:T(4,128)} %radiosity.1, f32[1,512]{1,0:T(1,128)} %bitcast.11, s32[1,512]{1,0:T(1,128)} %bitcast.12, f32[3,768]{1,0:T(4,128)} %position.1, f32[2,768]{1,0:T(2,128)} %angles.1, s32[1,128]{1,0:T(1,128)} %receiver.1, s32[1,128]{1,0:T(1,128)} %source.1, ...), custom_call_target="tpu_custom_call" | custom-call | tf_op jit(solution)/shard_map/pack/pallas_call | solution.py:422
  2.8 28.0 %all_to_all.15 = f32[16,5,4,128]{3,2,1,0:T(4,128)S(1)} all-to-all(f32[16,5,4,128]{3,2,1,0:T(4,128)} %get-tuple-element.10), channel_id=1, replica_groups=mesh['grp'=4,'dev_0'=16,'dev_1'=4,'dev_2'=2] {'dev_0'}, dimensions={0} | all-to-all | bytes 327680 | tf_op jit(solution)/shard_map/all_to_all | solution.py:441
  30.8 0.1 broadcast_in_dim.16
  30.9 0.0 copy-start.2
  30.9 11.6 %all_to_all.16 = f32[4,80,4,128]{3,2,1,0:T(4,128)S(1)} all-to-all(f32[4,80,4,128]{3,2,1,0:T(4,128)S(1)} %broadcast_in_dim.16), channel_id=1, replica_groups=mesh['grp'=4,'dev_0'=16,'dev_1'=4,'dev_2'=2] {'dev_1'}, dimensions={0} | all-to-all | bytes 1310720 | tf_op jit(solution)/shard_map/all_to_all | solution.py:442
  42.5 0.0 copy-done.2
  42.5 0.1 pad_maximum_fusion
  42.7 7.7 %collective-permute-start = (f32[332,4,128]{2,1,0:T(4,128)S(1)}, f32[332,4,128]{2,1,0:T(4,128)S(1)}, u32[]{:S(2)}, u32[]{:S(2)}) collective-permute-start(f32[332,4,128]{2,1,0:T(4,128)S(1)} %pad_maximum_fusion), channel_id=1, source_target_pairs={{0,1},{1,0},{2,3},{3,2},{4,5},{5,4},{6,7},{7,6},{8,9},{9,8},{10,11... | collective-permute-start | bytes 2039816 | tf_op jit(solution)/shard_map/ppermute | solution.py:446
  50.4 0.0 copy-start.1
  50.4 0.0 copy-start
  50.4 1.7 %collective-permute-done = f32[332,4,128]{2,1,0:T(4,128)S(1)} collective-permute-done((f32[332,4,128]{2,1,0:T(4,128)S(1)}, f32[332,4,128]{2,1,0:T(4,128)S(1)}, u32[]{:S(2)}, u32[]{:S(2)}) %collective-permute-start) | collective-permute-done | bytes 679968 | tf_op jit(solution)/shard_map/ppermute | solution.py:446
  52.1 0.0 copy-done.1
  52.1 0.0 copy-done
  52.1 13.2 %gather.1 = (f32[8,3,512]{2,1,0:T(4,128)S(1)}, f32[3,512]{1,0:T(4,128)S(1)}, f32[3,512]{1,0:T(4,128)S(1)}) custom-call(s32[1]{0:T(128)} %bitcast.where_ref, f32[1328,128]{1,0:T(8,128)S(1)} %bitcast.7, f32[1328,128]{1,0:T(8,128)S(1)} %bitcast.8, f32[3,512]{1,0:T(4,128)S(1)} %copy-done, f32[3,512]{1,0:T(4,128)S(1)} %copy-done.1), custom_call_target="tpu_custom_call" | custom-call | tf_op jit(solution)/shard_map/gather/pallas_call | solution.py:378
  65.3 9.0 %all_to_all.17 = f32[8,3,512]{2,1,0:T(4,128)S(1)} all-to-all(f32[8,3,512]{2,1,0:T(4,128)S(1)} %get-tuple-element.14), channel_id=1, replica_groups=mesh['grp'=4,'dev_0'=16,'dev_1'=4,'dev_2'=2] {'grp','dev_2'}, dimensions={0} | all-to-all | bytes 98304 | tf_op jit(solution)/shard_map/all_to_all | solution.py:459
  74.3 0.6 multiply_add_fusion
  (1 shorter events, 0.0 us)
Async XLA Ops:
  30.9 11.6 %copy-start.2 = (f32[12,4,128]{2,1,0:T(4,128)S(1)}, f32[12,4,128]{2,1,0:T(4,128)}, u32[]{:S(2)}) copy-start(f32[12,4,128]{2,1,0:T(4,128)} %get-tuple-element.11) | copy-start | bytes 73732
  42.7 9.5 %collective-permute-start = (f32[332,4,128]{2,1,0:T(4,128)S(1)}, f32[332,4,128]{2,1,0:T(4,128)S(1)}, u32[]{:S(2)}, u32[]{:S(2)}) collective-permute-start(f32[332,4,128]{2,1,0:T(4,128)S(1)} %pad_maximum_fusion), channel_id=1, source_target_pairs={{0,1},{1,0},{2,3},{3,2},{4,5},{5,4},{6,7},{7,6},{8,9},{9,8},{10,11... | collective-permute-start | bytes 2039816 | tf_op jit(solution)/shard_map/ppermute | solution.py:446
  50.4 1.7 %copy-start.1 = (f32[3,512]{1,0:T(4,128)S(1)}, f32[3,512]{1,0:T(4,128)}, u32[]{:S(2)}) copy-start(f32[3,512]{1,0:T(4,128)} %albedo_ref.1) | copy-start | bytes 18436
  50.4 1.7 %copy-start = (f32[3,512]{1,0:T(4,128)S(1)}, f32[3,512]{1,0:T(4,128)}, u32[]{:S(2)}) copy-start(f32[3,512]{1,0:T(4,128)} %emit_ref.1) | copy-start | bytes 18436

commit v4 on v3

--- a/solution.py
+++ b/solution.py
@@ -20,12 +20,19 @@
 OFFSETS = 248
 SHIFT = 1 << 13
 CHUNK = 512
-EXACT = lax.Precision.HIGHEST
 NT_DIMS = (((1,), (1,)), ((), ()))
 
 
 def lane_rows(array):
     return [array[:, at : at + TILE] for at in range(0, array.shape[1], TILE)]
+
+
+def terms(array, count):
+    parts = []
+    for _ in range(count):
+        parts.append(array.astype(jnp.bfloat16).astype(jnp.float32))
+        array = array - parts[-1]
+    return parts
 
 
 def pack_kernel(
@@ -40,14 +47,18 @@
     nodes = [position[a : a + 1, :] for a in range(3)]
     nodes += [jnp.cos(azimuth) * cos_e, jnp.sin(azimuth) * cos_e, jnp.sin(elevation)]
     clusters = lax.broadcasted_iota(jnp.int32, (cluster_count, leaf_count), 0)
-    onehot = (clusters == parent[...]).astype(jnp.float32)
+    onehot = (clusters == parent[...]).astype(jnp.bfloat16)
     leaf_area = area[...]
     values = jnp.concatenate(
         [leaf_area, radiosity[...] * leaf_area, jnp.zeros((4, leaf_count), jnp.float32)], axis=0
     )
     sums = lax.dot_general(
-        values, onehot, NT_DIMS, precision=EXACT, preferred_element_type=jnp.float32
-    )
+        jnp.concatenate(terms(values, 3), axis=0).astype(jnp.bfloat16),
+        onehot,
+        NT_DIMS,
+        preferred_element_type=jnp.float32,
+    )
+    sums = sums[0:8, :] + sums[8:16, :] + sums[16:24, :]
     cluster_area = sums[0:1, :]
     cluster_radiosity = sums[1:4, :] / cluster_area
     scale = cluster_area * (-1.0 / math.pi)
@@ -59,8 +70,8 @@
     before = (
         lax.broadcasted_iota(jnp.int32, (slots, slots), 0)
         < lax.broadcasted_iota(jnp.int32, (slots, slots), 1)
-    ).astype(jnp.float32)
-    place = jnp.dot(member, before, preferred_element_type=jnp.float32)
+    ).astype(jnp.bfloat16)
+    place = jnp.dot(member.astype(jnp.bfloat16), before, preferred_element_type=jnp.float32)
     held = jnp.sum(member, axis=1, keepdims=True)
     quads = jnp.broadcast_to(jnp.floor((held + (QUAD - 1)) * (1.0 / QUAD)), (8, slots))
     first = jnp.zeros((8, slots), jnp.float32)
@@ -71,8 +82,9 @@
     spot = jnp.sum(member * (first + quad + turn * QUADS), axis=0, keepdims=True)
     alive = jnp.sum(member, axis=0, keepdims=True)
     spot = jnp.where(alive > 0.0, spot, -1.0).astype(jnp.int32)
-    to_spot = (lax.broadcasted_iota(jnp.int32, (2 * slots, slots), 0) == spot).astype(jnp.float32)
+    to_spot = (lax.broadcasted_iota(jnp.int32, (2 * slots, slots), 0) == spot).astype(jnp.bfloat16)
     entries = jnp.broadcast_to((source[...] + 1).astype(jnp.float32), (8, slots))
+    entries = entries.astype(jnp.bfloat16)
     ordered = lax.dot_general(entries, to_spot, NT_DIMS, preferred_element_type=jnp.float32)
     offsets = jnp.sum(
         jnp.where(lanes == OFFSETS - TILE + tiles, first, 0.0), axis=0, keepdims=True
@@ -313,22 +325,15 @@
     lax.fori_loop(1, (table[QUAD + 2, 0] + CHUNK - 1) // CHUNK, next_chunk, acc)
 
     places = shards * 8
-    ones = jnp.ones((8, TILE), jnp.float32)
-    parts = []
+    band = lax.broadcasted_iota(jnp.int32, (TILE, TILE), 1)
+    sums = jnp.zeros((places, TILE), jnp.float32)
     for c in range(3):
-        left = lax.dot_general(
-            ones,
-            totals[c, 0:places, :],
-            NT_DIMS,
-            precision=EXACT,
-            preferred_element_type=jnp.float32,
-        )[0:1, :]
-        for _ in range(3):
-            near = left.astype(jnp.bfloat16)
-            parts.append(near.astype(jnp.float32))
-            left = left - parts[-1]
-    parts = jnp.concatenate(parts + [jnp.zeros((7, places), jnp.float32)], axis=0)
-    parts = parts.astype(jnp.bfloat16)
+        to_band = (band == c).astype(jnp.bfloat16)
+        for part in terms(totals[c, 0:places, :], 2):
+            sums = sums + jnp.dot(
+                part.astype(jnp.bfloat16), to_band, preferred_element_type=jnp.float32
+            )
+    parts = jnp.concatenate(terms(sums.T[0:8, :], 2), axis=0).astype(jnp.bfloat16)
     place = lax.broadcasted_iota(jnp.int32, (places, TILE), 0)
     lane = lax.broadcasted_iota(jnp.int32, (places, TILE), 1)
     link = place >> 3
@@ -343,12 +348,7 @@
             sums = jnp.dot(
                 parts, picked.astype(jnp.bfloat16), preferred_element_type=jnp.float32
             )
-            pieces.append(
-                jnp.concatenate(
-                    [sums[3 * c : 3 * c + 1] + sums[3 * c + 1 : 3 * c + 2] + sums[3 * c + 2 : 3 * c + 3] for c in range(3)],
-                    axis=0,
-                )
-            )
+            pieces.append(sums[0:3, :] + sums[8:11, :])
         return jnp.concatenate(pieces, axis=1)
 
     first_slot = jnp.where(late, split, 0)

time: 75.3 us -> 74.4 us (0.988)
  Pallas kernels: 15.4 us -> 14.4 us
where the time goes in v4:
time: 74.4 us; the launch traced here: 74.1 us
  blocking collectives  48.6 us (65%)
  Pallas kernels  14.4 us (19%)
  starting transfers between devices  7.71 us (10%)
  waiting for transfers between devices  1.71 us (2%)
  other arithmetic  0.78 us (1%)
    all_to_all x1, blocking collectives, body(): held = lax.all_to_all(held, DEV[0], 0, 0, tiled=True).reshape(-1, 4, TILE)  28 us
    pallas_call x1, Pallas kernels, gather_call(): pl.pallas_call(functools.partial(gather_kernel, sizes=sizes, node_count=n...  12.6 us
    all_to_all x1, blocking collectives, body(): lax.all_to_all(jnp.broadcast_to(held[None], (sizes[1], *held.shape)), DEV...  11.6 us
    all_to_all x1, blocking collectives, body(): lax.all_to_all(partial, ('grp', DEV[2]), 0, 0, tiled=True).sum(axis=0)  9.06 us
    ppermute x1, starting transfers between devices, body(): other = lax.ppermute(held, DEV[2], [(0, 1), (1, 0)])  7.71 us
    pallas_call x1, Pallas kernels, body(): pl.pallas_call(pack_kernel, out_shape=(jax.ShapeDtypeStruct((sizes[0], PA...  1.82 us
    ppermute x1, waiting for transfers between devices, body(): other = lax.ppermute(held, DEV[2], [(0, 1), (1, 0)])  1.71 us
  transfers between devices with their start and end apart: 1, of which 1 were waited for; matrix products, arithmetic and copies ran while one was open for 0% of the time, Pallas kernels for 0%

profile of v4, /device:TPU:1, one launch (start us, length us, event | category | flops | bytes accessed | tf_op | source)
XLA Modules:
  0.0 74.1 jit_solution(8748725836561719825)
XLA Ops:
  0.7 1.8 %pack.1 = (f32[16,5,4,128]{3,2,1,0:T(4,128)}, f32[12,4,128]{2,1,0:T(4,128)}) custom-call(f32[3,512]{1,0:T(4,128)} %radiosity.1, f32[1,512]{1,0:T(1,128)} %bitcast.11, s32[1,512]{1,0:T(1,128)} %bitcast.12, f32[3,768]{1,0:T(4,128)} %position.1, f32[2,768]{1,0:T(2,128)} %angles.1, s32[1,128]{1,0:T(1,128)} %receiver.1, s32[1,128]{1,0:T(1,128)} %source.1, ...), custom_call_target="tpu_custom_call" | custom-call | tf_op jit(solution)/shard_map/pack/pallas_call | solution.py:422
  2.5 28.0 %all_to_all.15 = f32[16,5,4,128]{3,2,1,0:T(4,128)S(1)} all-to-all(f32[16,5,4,128]{3,2,1,0:T(4,128)} %get-tuple-element.10), channel_id=1, replica_groups=mesh['grp'=4,'dev_0'=16,'dev_1'=4,'dev_2'=2] {'dev_0'}, dimensions={0} | all-to-all | bytes 327680 | tf_op jit(solution)/shard_map/all_to_all | solution.py:441
  30.4 0.1 broadcast_in_dim.16
  30.5 0.0 copy-start.2
  30.5 11.6 %all_to_all.16 = f32[4,80,4,128]{3,2,1,0:T(4,128)S(1)} all-to-all(f32[4,80,4,128]{3,2,1,0:T(4,128)S(1)} %broadcast_in_dim.16), channel_id=1, replica_groups=mesh['grp'=4,'dev_0'=16,'dev_1'=4,'dev_2'=2] {'dev_1'}, dimensions={0} | all-to-all | bytes 1310720 | tf_op jit(solution)/shard_map/all_to_all | solution.py:442
  42.2 0.0 copy-done.2
  42.2 0.1 pad_maximum_fusion
  42.3 7.7 %collective-permute-start = (f32[332,4,128]{2,1,0:T(4,128)S(1)}, f32[332,4,128]{2,1,0:T(4,128)S(1)}, u32[]{:S(2)}, u32[]{:S(2)}) collective-permute-start(f32[332,4,128]{2,1,0:T(4,128)S(1)} %pad_maximum_fusion), channel_id=1, source_target_pairs={{0,1},{1,0},{2,3},{3,2},{4,5},{5,4},{6,7},{7,6},{8,9},{9,8},{10,11... | collective-permute-start | bytes 2039816 | tf_op jit(solution)/shard_map/ppermute | solution.py:446
  50.0 0.0 copy-start.1
  50.0 0.0 copy-start
  50.1 1.7 %collective-permute-done = f32[332,4,128]{2,1,0:T(4,128)S(1)} collective-permute-done((f32[332,4,128]{2,1,0:T(4,128)S(1)}, f32[332,4,128]{2,1,0:T(4,128)S(1)}, u32[]{:S(2)}, u32[]{:S(2)}) %collective-permute-start) | collective-permute-done | bytes 679968 | tf_op jit(solution)/shard_map/ppermute | solution.py:446
  51.8 0.0 copy-done.1
  51.8 0.0 copy-done
  51.8 12.6 %gather.1 = (f32[8,3,512]{2,1,0:T(4,128)S(1)}, f32[3,512]{1,0:T(4,128)S(1)}, f32[3,512]{1,0:T(4,128)S(1)}) custom-call(s32[1]{0:T(128)} %bitcast.where_ref, f32[1328,128]{1,0:T(8,128)S(1)} %bitcast.7, f32[1328,128]{1,0:T(8,128)S(1)} %bitcast.8, f32[3,512]{1,0:T(4,128)S(1)} %copy-done, f32[3,512]{1,0:T(4,128)S(1)} %copy-done.1), custom_call_target="tpu_custom_call" | custom-call | tf_op jit(solution)/shard_map/gather/pallas_call | solution.py:378
  64.4 9.1 %all_to_all.17 = f32[8,3,512]{2,1,0:T(4,128)S(1)} all-to-all(f32[8,3,512]{2,1,0:T(4,128)S(1)} %get-tuple-element.14), channel_id=1, replica_groups=mesh['grp'=4,'dev_0'=16,'dev_1'=4,'dev_2'=2] {'grp','dev_2'}, dimensions={0} | all-to-all | bytes 98304 | tf_op jit(solution)/shard_map/all_to_all | solution.py:459
  73.5 0.6 multiply_add_fusion
  (1 shorter events, 0.0 us)
Async XLA Ops:
  30.5 11.6 %copy-start.2 = (f32[12,4,128]{2,1,0:T(4,128)S(1)}, f32[12,4,128]{2,1,0:T(4,128)}, u32[]{:S(2)}) copy-start(f32[12,4,128]{2,1,0:T(4,128)} %get-tuple-element.11) | copy-start | bytes 73732
  42.3 9.5 %collective-permute-start = (f32[332,4,128]{2,1,0:T(4,128)S(1)}, f32[332,4,128]{2,1,0:T(4,128)S(1)}, u32[]{:S(2)}, u32[]{:S(2)}) collective-permute-start(f32[332,4,128]{2,1,0:T(4,128)S(1)} %pad_maximum_fusion), channel_id=1, source_target_pairs={{0,1},{1,0},{2,3},{3,2},{4,5},{5,4},{6,7},{7,6},{8,9},{9,8},{10,11... | collective-permute-start | bytes 2039816 | tf_op jit(solution)/shard_map/ppermute | solution.py:446
  50.0 1.7 %copy-start.1 = (f32[3,512]{1,0:T(4,128)S(1)}, f32[3,512]{1,0:T(4,128)}, u32[]{:S(2)}) copy-start(f32[3,512]{1,0:T(4,128)} %albedo_ref.1) | copy-start | bytes 18436
  50.0 1.7 %copy-start = (f32[3,512]{1,0:T(4,128)S(1)}, f32[3,512]{1,0:T(4,128)}, u32[]{:S(2)}) copy-start(f32[3,512]{1,0:T(4,128)} %emit_ref.1) | copy-start | bytes 18436

commit v5 on v4

--- a/solution.py
+++ b/solution.py
@@ -11,15 +11,15 @@
 
 TILE = 128
 DEV = ("dev_0", "dev_1", "dev_2")
-QUAD = 4
-QUADS = 40
-STEP = 4
+RUN = 3
+RUNS = 48
+STEP = 8
 PACK = 20
 FIELDS = 9
 SOURCE = 16
 OFFSETS = 248
 SHIFT = 1 << 13
-CHUNK = 512
+CHUNK = 640
 NT_DIMS = (((1,), (1,)), ((), ()))
 
 
@@ -41,11 +41,11 @@
     leaf_count = area.shape[1]
     node_count = position.shape[1]
     cluster_count = node_count - leaf_count
-    azimuth = angles[0:1, :]
-    elevation = angles[1:2, :]
-    cos_e = jnp.cos(elevation)
+    sines = jnp.sin(angles[...])
+    cosines = jnp.cos(angles[...])
+    cos_e = cosines[1:2, :]
     nodes = [position[a : a + 1, :] for a in range(3)]
-    nodes += [jnp.cos(azimuth) * cos_e, jnp.sin(azimuth) * cos_e, jnp.sin(elevation)]
+    nodes += [cosines[0:1, :] * cos_e, sines[0:1, :] * cos_e, sines[1:2, :]]
     clusters = lax.broadcasted_iota(jnp.int32, (cluster_count, leaf_count), 0)
     onehot = (clusters == parent[...]).astype(jnp.bfloat16)
     leaf_area = area[...]
@@ -73,13 +73,13 @@
     ).astype(jnp.bfloat16)
     place = jnp.dot(member.astype(jnp.bfloat16), before, preferred_element_type=jnp.float32)
     held = jnp.sum(member, axis=1, keepdims=True)
-    quads = jnp.broadcast_to(jnp.floor((held + (QUAD - 1)) * (1.0 / QUAD)), (8, slots))
+    runs = jnp.broadcast_to(jnp.floor((held + (RUN - 0.5)) * (1.0 / RUN)), (8, slots))
     first = jnp.zeros((8, slots), jnp.float32)
     for t in range(7):
-        first = first + jnp.where(tiles > t, quads[t : t + 1, :], 0.0)
-    quad = jnp.floor(place * (1.0 / QUAD))
-    turn = place - quad * QUAD
-    spot = jnp.sum(member * (first + quad + turn * QUADS), axis=0, keepdims=True)
+        first = first + jnp.where(tiles > t, runs[t : t + 1, :], 0.0)
+    run = jnp.floor((place + 0.5) * (1.0 / RUN))
+    turn = place - run * RUN
+    spot = jnp.sum(member * (first + run + turn * RUNS), axis=0, keepdims=True)
     alive = jnp.sum(member, axis=0, keepdims=True)
     spot = jnp.where(alive > 0.0, spot, -1.0).astype(jnp.int32)
     to_spot = (lax.broadcasted_iota(jnp.int32, (2 * slots, slots), 0) == spot).astype(jnp.bfloat16)
@@ -196,19 +196,19 @@
             listed, chosen, (((0,), (0,)), ((), ())), preferred_element_type=jnp.float32
         )
         owner = found[OFFSETS : OFFSETS + 1, :].astype(jnp.int32)
-        quad = found[OFFSETS + 1 : OFFSETS + 2, :] * TILE + found[OFFSETS + 2 : OFFSETS + 3, :]
-        quad = quad - SHIFT + place
-        goes_on = jnp.where(quad > found[OFFSETS + 3 : OFFSETS + 4, :], 1, 0)
-        quads = lax.broadcasted_iota(jnp.int32, (QUADS, CHUNK), 0).astype(jnp.float32)
-        match = quads == quad
+        run = found[OFFSETS + 1 : OFFSETS + 2, :] * TILE + found[OFFSETS + 2 : OFFSETS + 3, :]
+        run = run - SHIFT + place
+        goes_on = jnp.where(run > found[OFFSETS + 3 : OFFSETS + 4, :], 1, 0)
+        runs = lax.broadcasted_iota(jnp.int32, (RUNS, CHUNK), 0).astype(jnp.float32)
+        match = runs == run
         entries = jnp.concatenate(
             [
                 jnp.sum(
-                    jnp.where(match, found[u * QUADS : (u + 1) * QUADS, :], 0.0),
+                    jnp.where(match, found[u * RUNS : (u + 1) * RUNS, :], 0.0),
                     axis=0,
                     keepdims=True,
                 )
-                for u in range(QUAD)
+                for u in range(RUN)
             ],
             axis=0,
         ).astype(jnp.int32)
@@ -229,7 +229,7 @@
         total = total.astype(jnp.int32)
         link = jnp.where(spot < total, link, shards) * 8
         table_vmem[...] = jnp.concatenate(
-            [rows, link, goes_on, total, jnp.zeros((1, CHUNK), jnp.int32)], axis=0
+            [rows, link, goes_on, total, jnp.zeros((5 - RUN, CHUNK), jnp.int32)], axis=0
         )
         return pltpu.make_async_copy(table_vmem, table, sem)
 
@@ -291,11 +291,11 @@
     def step(turn, acc):
         for n in range(STEP):
             spot = turn * STEP + n
-            at = pl.ds(pl.multiple_of(table[QUAD, spot], 8), 8)
-            keep = jnp.where(table[QUAD + 1, spot] > 0, 1.0, 0.0)
+            at = pl.ds(pl.multiple_of(table[RUN, spot], 8), 8)
+            keep = jnp.where(table[RUN + 1, spot] > 0, 1.0, 0.0)
             rec = [receivers[field, at, :] for field in range(6)]
             acc = [a * keep for a in acc]
-            for u in range(QUAD):
+            for u in range(RUN):
                 row = pl.multiple_of(table[u, spot], SOURCE)
                 src = [sources[pl.ds(row + f, 1), :] for f in range(FIELDS + 2)]
                 d = [src[a] - rec[a] for a in range(3)]
@@ -310,7 +310,7 @@
         return acc
 
     def work_off(chunk, acc):
-        held = jnp.clip(table[QUAD + 2, 0] - chunk * CHUNK, 0, CHUNK)
+        held = jnp.clip(table[RUN + 2, 0] - chunk * CHUNK, 0, CHUNK)
         return lax.fori_loop(0, (held + STEP - 1) // STEP, step, acc)
 
     def next_chunk(chunk, acc):
@@ -322,17 +322,18 @@
     zero = jnp.zeros((8, TILE), jnp.float32)
     fetch.wait()
     acc = work_off(0, [zero] * 3)
-    lax.fori_loop(1, (table[QUAD + 2, 0] + CHUNK - 1) // CHUNK, next_chunk, acc)
+    lax.fori_loop(1, (table[RUN + 2, 0] + CHUNK - 1) // CHUNK, next_chunk, acc)
 
     places = shards * 8
     band = lax.broadcasted_iota(jnp.int32, (TILE, TILE), 1)
     sums = jnp.zeros((places, TILE), jnp.float32)
     for c in range(3):
         to_band = (band == c).astype(jnp.bfloat16)
-        for part in terms(totals[c, 0:places, :], 2):
-            sums = sums + jnp.dot(
-                part.astype(jnp.bfloat16), to_band, preferred_element_type=jnp.float32
-            )
+        whole = totals[c, 0:places, :]
+        near = whole.astype(jnp.bfloat16)
+        rest = (whole - near.astype(jnp.float32)).astype(jnp.bfloat16)
+        for part in (near, rest):
+            sums = sums + jnp.dot(part, to_band, preferred_element_type=jnp.float32)
     parts = jnp.concatenate(terms(sums.T[0:8, :], 2), axis=0).astype(jnp.bfloat16)
     place = lax.broadcasted_iota(jnp.int32, (places, TILE), 0)
     lane = lax.broadcasted_iota(jnp.int32, (places, TILE), 1)
@@ -344,7 +345,7 @@
         for chunk in range(leaf_count // TILE):
             parent = ref[pl.ds(local + 6 * chunks + chunk, 1), :].astype(jnp.int32) + leaf_count
             leaf = lane + chunk * TILE
-            picked = jnp.where(node == leaf, 1.0, 0.0) + jnp.where(node == parent, 1.0, 0.0)
+            picked = jnp.where((node == leaf) | (node == parent), 1.0, 0.0)
             sums = jnp.dot(
                 parts, picked.astype(jnp.bfloat16), preferred_element_type=jnp.float32
             )

time: 74.4 us -> 74.2 us (level)
  no operation moved by 1% of the time
where the time goes in v5:
time: 74.2 us; the launch traced here: 73.9 us
  blocking collectives  49 us (66%)
  Pallas kernels  13.9 us (19%)
  starting transfers between devices  7.71 us (10%)
  waiting for transfers between devices  1.71 us (2%)
  other arithmetic  0.78 us (1%)
    all_to_all x1, blocking collectives, body(): held = lax.all_to_all(held, DEV[0], 0, 0, tiled=True).reshape(-1, 4, TILE)  28 us
    pallas_call x1, Pallas kernels, gather_call(): pl.pallas_call(functools.partial(gather_kernel, sizes=sizes, node_count=n...  12.1 us
    all_to_all x1, blocking collectives, body(): lax.all_to_all(jnp.broadcast_to(held[None], (sizes[1], *held.shape)), DEV...  11.6 us
    all_to_all x1, blocking collectives, body(): lax.all_to_all(partial, ('grp', DEV[2]), 0, 0, tiled=True).sum(axis=0)  9.43 us
    ppermute x1, starting transfers between devices, body(): other = lax.ppermute(held, DEV[2], [(0, 1), (1, 0)])  7.71 us
    pallas_call x1, Pallas kernels, body(): pl.pallas_call(pack_kernel, out_shape=(jax.ShapeDtypeStruct((sizes[0], PA...  1.82 us
    ppermute x1, waiting for transfers between devices, body(): other = lax.ppermute(held, DEV[2], [(0, 1), (1, 0)])  1.71 us
  transfers between devices with their start and end apart: 1, of which 1 were waited for; matrix products, arithmetic and copies ran while one was open for 0% of the time, Pallas kernels for 0%

profile of v5, /device:TPU:1, one launch (start us, length us, event | category | flops | bytes accessed | tf_op | source)
XLA Modules:
  0.0 73.9 jit_solution(14223611768020434442)
XLA Ops:
  0.7 1.8 %pack.1 = (f32[16,5,4,128]{3,2,1,0:T(4,128)}, f32[12,4,128]{2,1,0:T(4,128)}) custom-call(f32[3,512]{1,0:T(4,128)} %radiosity.1, f32[1,512]{1,0:T(1,128)} %bitcast.11, s32[1,512]{1,0:T(1,128)} %bitcast.12, f32[3,768]{1,0:T(4,128)} %position.1, f32[2,768]{1,0:T(2,128)} %angles.1, s32[1,128]{1,0:T(1,128)} %receiver.1, s32[1,128]{1,0:T(1,128)} %source.1, ...), custom_call_target="tpu_custom_call" | custom-call | tf_op jit(solution)/shard_map/pack/pallas_call | solution.py:423
  2.5 28.0 %all_to_all.15 = f32[16,5,4,128]{3,2,1,0:T(4,128)S(1)} all-to-all(f32[16,5,4,128]{3,2,1,0:T(4,128)} %get-tuple-element.10), channel_id=1, replica_groups=mesh['grp'=4,'dev_0'=16,'dev_1'=4,'dev_2'=2] {'dev_0'}, dimensions={0} | all-to-all | bytes 327680 | tf_op jit(solution)/shard_map/all_to_all | solution.py:442
  30.4 0.1 broadcast_in_dim.16
  30.5 0.0 copy-start.2
  30.5 11.6 %all_to_all.16 = f32[4,80,4,128]{3,2,1,0:T(4,128)S(1)} all-to-all(f32[4,80,4,128]{3,2,1,0:T(4,128)S(1)} %broadcast_in_dim.16), channel_id=1, replica_groups=mesh['grp'=4,'dev_0'=16,'dev_1'=4,'dev_2'=2] {'dev_1'}, dimensions={0} | all-to-all | bytes 1310720 | tf_op jit(solution)/shard_map/all_to_all | solution.py:443
  42.2 0.0 copy-done.2
  42.2 0.1 pad_maximum_fusion
  42.3 7.7 %collective-permute-start = (f32[332,4,128]{2,1,0:T(4,128)S(1)}, f32[332,4,128]{2,1,0:T(4,128)S(1)}, u32[]{:S(2)}, u32[]{:S(2)}) collective-permute-start(f32[332,4,128]{2,1,0:T(4,128)S(1)} %pad_maximum_fusion), channel_id=1, source_target_pairs={{0,1},{1,0},{2,3},{3,2},{4,5},{5,4},{6,7},{7,6},{8,9},{9,8},{10,11... | collective-permute-start | bytes 2039816 | tf_op jit(solution)/shard_map/ppermute | solution.py:447
  50.0 0.0 copy-start.1
  50.0 0.0 copy-start
  50.1 1.7 %collective-permute-done = f32[332,4,128]{2,1,0:T(4,128)S(1)} collective-permute-done((f32[332,4,128]{2,1,0:T(4,128)S(1)}, f32[332,4,128]{2,1,0:T(4,128)S(1)}, u32[]{:S(2)}, u32[]{:S(2)}) %collective-permute-start) | collective-permute-done | bytes 679968 | tf_op jit(solution)/shard_map/ppermute | solution.py:447
  51.8 0.0 copy-done.1
  51.8 0.0 copy-done
  51.8 12.1 %gather.1 = (f32[8,3,512]{2,1,0:T(4,128)S(1)}, f32[3,512]{1,0:T(4,128)S(1)}, f32[3,512]{1,0:T(4,128)S(1)}) custom-call(s32[1]{0:T(128)} %bitcast.where_ref, f32[1328,128]{1,0:T(8,128)S(1)} %bitcast.7, f32[1328,128]{1,0:T(8,128)S(1)} %bitcast.8, f32[3,512]{1,0:T(4,128)S(1)} %copy-done, f32[3,512]{1,0:T(4,128)S(1)} %copy-done.1), custom_call_target="tpu_custom_call" | custom-call | tf_op jit(solution)/shard_map/gather/pallas_call | solution.py:379
  63.9 9.4 %all_to_all.17 = f32[8,3,512]{2,1,0:T(4,128)S(1)} all-to-all(f32[8,3,512]{2,1,0:T(4,128)S(1)} %get-tuple-element.14), channel_id=1, replica_groups=mesh['grp'=4,'dev_0'=16,'dev_1'=4,'dev_2'=2] {'grp','dev_2'}, dimensions={0} | all-to-all | bytes 98304 | tf_op jit(solution)/shard_map/all_to_all | solution.py:460
  73.3 0.6 multiply_add_fusion
  (1 shorter events, 0.0 us)
Async XLA Ops:
  30.5 11.6 %copy-start.2 = (f32[12,4,128]{2,1,0:T(4,128)S(1)}, f32[12,4,128]{2,1,0:T(4,128)}, u32[]{:S(2)}) copy-start(f32[12,4,128]{2,1,0:T(4,128)} %get-tuple-element.11) | copy-start | bytes 73732
  42.3 9.5 %collective-permute-start = (f32[332,4,128]{2,1,0:T(4,128)S(1)}, f32[332,4,128]{2,1,0:T(4,128)S(1)}, u32[]{:S(2)}, u32[]{:S(2)}) collective-permute-start(f32[332,4,128]{2,1,0:T(4,128)S(1)} %pad_maximum_fusion), channel_id=1, source_target_pairs={{0,1},{1,0},{2,3},{3,2},{4,5},{5,4},{6,7},{7,6},{8,9},{9,8},{10,11... | collective-permute-start | bytes 2039816 | tf_op jit(solution)/shard_map/ppermute | solution.py:447
  50.0 1.7 %copy-start.1 = (f32[3,512]{1,0:T(4,128)S(1)}, f32[3,512]{1,0:T(4,128)}, u32[]{:S(2)}) copy-start(f32[3,512]{1,0:T(4,128)} %albedo_ref.1) | copy-start | bytes 18436
  50.0 1.7 %copy-start = (f32[3,512]{1,0:T(4,128)S(1)}, f32[3,512]{1,0:T(4,128)}, u32[]{:S(2)}) copy-start(f32[3,512]{1,0:T(4,128)} %emit_ref.1) | copy-start | bytes 18436

commit v6 on v5

--- a/solution.py
+++ b/solution.py
@@ -13,7 +13,7 @@
 DEV = ("dev_0", "dev_1", "dev_2")
 RUN = 3
 RUNS = 48
-STEP = 8
+STEP = 16
 PACK = 20
 FIELDS = 9
 SOURCE = 16
@@ -177,7 +177,7 @@
     shift = first - ahead + SHIFT
     coarse = jnp.floor(shift * (1.0 / TILE))
     high = jnp.where(lane < OFFSETS - TILE, high, 0.0)
-    extras = (arrival.astype(jnp.float32), coarse, shift - coarse * TILE, first)
+    extras = (arrival.astype(jnp.float32), coarse, shift - coarse * TILE)
     for n, extra in enumerate(extras):
         high = jnp.where(lane == OFFSETS - TILE + n, extra, high)
     listed = jnp.concatenate([low, high], axis=1).astype(jnp.bfloat16)
@@ -198,7 +198,6 @@
         owner = found[OFFSETS : OFFSETS + 1, :].astype(jnp.int32)
         run = found[OFFSETS + 1 : OFFSETS + 2, :] * TILE + found[OFFSETS + 2 : OFFSETS + 3, :]
         run = run - SHIFT + place
-        goes_on = jnp.where(run > found[OFFSETS + 3 : OFFSETS + 4, :], 1, 0)
         runs = lax.broadcasted_iota(jnp.int32, (RUNS, CHUNK), 0).astype(jnp.float32)
         match = runs == run
         entries = jnp.concatenate(
@@ -229,7 +228,7 @@
         total = total.astype(jnp.int32)
         link = jnp.where(spot < total, link, shards) * 8
         table_vmem[...] = jnp.concatenate(
-            [rows, link, goes_on, total, jnp.zeros((5 - RUN, CHUNK), jnp.int32)], axis=0
+            [rows, link, total, jnp.zeros((6 - RUN, CHUNK), jnp.int32)], axis=0
         )
         return pltpu.make_async_copy(table_vmem, table, sem)
 
@@ -288,13 +287,12 @@
     for c in range(3):
         totals[c, :, :] = jnp.zeros(((shards + 8) * 8, TILE), jnp.float32)
 
-    def step(turn, acc):
+    def step(turn, carry):
         for n in range(STEP):
             spot = turn * STEP + n
             at = pl.ds(pl.multiple_of(table[RUN, spot], 8), 8)
-            keep = jnp.where(table[RUN + 1, spot] > 0, 1.0, 0.0)
             rec = [receivers[field, at, :] for field in range(6)]
-            acc = [a * keep for a in acc]
+            acc = None
             for u in range(RUN):
                 row = pl.multiple_of(table[u, spot], SOURCE)
                 src = [sources[pl.ds(row + f, 1), :] for f in range(FIELDS + 2)]
@@ -304,25 +302,26 @@
                 back = src[3] * d[0] + src[4] * d[1] + src[5] * d[2]
                 top = jnp.maximum(toward, 0.0) * jnp.maximum(back, 0.0)
                 factor = top / ((r2 + src[9]) * (r2 + src[10]))
-                acc = [acc[c] + factor * src[6 + c] for c in range(3)]
+                more = [factor * src[6 + c] for c in range(3)]
+                acc = more if acc is None else [acc[c] + more[c] for c in range(3)]
             for c in range(3):
-                totals[c, at, :] = acc[c]
-        return acc
-
-    def work_off(chunk, acc):
-        held = jnp.clip(table[RUN + 2, 0] - chunk * CHUNK, 0, CHUNK)
-        return lax.fori_loop(0, (held + STEP - 1) // STEP, step, acc)
-
-    def next_chunk(chunk, acc):
+                totals[c, at, :] = totals[c, at, :] + acc[c]
+        return carry
+
+    def work_off(chunk):
+        held = jnp.clip(table[RUN + 1, 0] - chunk * CHUNK, 0, CHUNK)
+        lax.fori_loop(0, (held + STEP - 1) // STEP, step, 0)
+
+    def next_chunk(chunk, carry):
         again = lay_out(chunk)
         again.start()
         again.wait()
-        return work_off(chunk, acc)
-
-    zero = jnp.zeros((8, TILE), jnp.float32)
+        work_off(chunk)
+        return carry
+
     fetch.wait()
-    acc = work_off(0, [zero] * 3)
-    lax.fori_loop(1, (table[RUN + 2, 0] + CHUNK - 1) // CHUNK, next_chunk, acc)
+    work_off(0)
+    lax.fori_loop(1, (table[RUN + 1, 0] + CHUNK - 1) // CHUNK, next_chunk, 0)
 
     places = shards * 8
     band = lax.broadcasted_iota(jnp.int32, (TILE, TILE), 1)

time: 74.2 us -> 73.9 us (level)
  no operation moved by 1% of the time
where the time goes in v6:
time: 73.9 us; the launch traced here: 73.5 us
  blocking collectives  48.9 us (66%)
  Pallas kernels  13.5 us (18%)
  starting transfers between devices  7.71 us (10%)
  waiting for transfers between devices  1.71 us (2%)
  other arithmetic  0.78 us (1%)
    all_to_all x1, blocking collectives, body(): held = lax.all_to_all(held, DEV[0], 0, 0, tiled=True).reshape(-1, 4, TILE)  28 us
    pallas_call x1, Pallas kernels, gather_call(): pl.pallas_call(functools.partial(gather_kernel, sizes=sizes, node_count=n...  11.7 us
    all_to_all x1, blocking collectives, body(): lax.all_to_all(jnp.broadcast_to(held[None], (sizes[1], *held.shape)), DEV...  11.6 us
    all_to_all x1, blocking collectives, body(): lax.all_to_all(partial, ('grp', DEV[2]), 0, 0, tiled=True).sum(axis=0)  9.34 us
    ppermute x1, starting transfers between devices, body(): other = lax.ppermute(held, DEV[2], [(0, 1), (1, 0)])  7.71 us
    pallas_call x1, Pallas kernels, body(): pl.pallas_call(pack_kernel, out_shape=(jax.ShapeDtypeStruct((sizes[0], PA...  1.82 us
    ppermute x1, waiting for transfers between devices, body(): other = lax.ppermute(held, DEV[2], [(0, 1), (1, 0)])  1.71 us
  transfers between devices with their start and end apart: 1, of which 1 were waited for; matrix products, arithmetic and copies ran while one was open for 0% of the time, Pallas kernels for 0%

profile of v6, /device:TPU:1, one launch (start us, length us, event | category | flops | bytes accessed | tf_op | source)
XLA Modules:
  0.0 73.5 jit_solution(16063806138925926046)
XLA Ops:
  0.7 1.8 %pack.1 = (f32[16,5,4,128]{3,2,1,0:T(4,128)}, f32[12,4,128]{2,1,0:T(4,128)}) custom-call(f32[3,512]{1,0:T(4,128)} %radiosity.1, f32[1,512]{1,0:T(1,128)} %bitcast.11, s32[1,512]{1,0:T(1,128)} %bitcast.12, f32[3,768]{1,0:T(4,128)} %position.1, f32[2,768]{1,0:T(2,128)} %angles.1, s32[1,128]{1,0:T(1,128)} %receiver.1, s32[1,128]{1,0:T(1,128)} %source.1, ...), custom_call_target="tpu_custom_call" | custom-call | tf_op jit(solution)/shard_map/pack/pallas_call | solution.py:422
  2.5 28.0 %all_to_all.15 = f32[16,5,4,128]{3,2,1,0:T(4,128)S(1)} all-to-all(f32[16,5,4,128]{3,2,1,0:T(4,128)} %get-tuple-element.10), channel_id=1, replica_groups=mesh['grp'=4,'dev_0'=16,'dev_1'=4,'dev_2'=2] {'dev_0'}, dimensions={0} | all-to-all | bytes 327680 | tf_op jit(solution)/shard_map/all_to_all | solution.py:441
  30.4 0.1 broadcast_in_dim.16
  30.5 0.0 copy-start.2
  30.5 11.6 %all_to_all.16 = f32[4,80,4,128]{3,2,1,0:T(4,128)S(1)} all-to-all(f32[4,80,4,128]{3,2,1,0:T(4,128)S(1)} %broadcast_in_dim.16), channel_id=1, replica_groups=mesh['grp'=4,'dev_0'=16,'dev_1'=4,'dev_2'=2] {'dev_1'}, dimensions={0} | all-to-all | bytes 1310720 | tf_op jit(solution)/shard_map/all_to_all | solution.py:442
  42.2 0.0 copy-done.2
  42.2 0.1 pad_maximum_fusion
  42.3 7.7 %collective-permute-start = (f32[332,4,128]{2,1,0:T(4,128)S(1)}, f32[332,4,128]{2,1,0:T(4,128)S(1)}, u32[]{:S(2)}, u32[]{:S(2)}) collective-permute-start(f32[332,4,128]{2,1,0:T(4,128)S(1)} %pad_maximum_fusion), channel_id=1, source_target_pairs={{0,1},{1,0},{2,3},{3,2},{4,5},{5,4},{6,7},{7,6},{8,9},{9,8},{10,11... | collective-permute-start | bytes 2039816 | tf_op jit(solution)/shard_map/ppermute | solution.py:446
  50.0 0.0 copy-start.1
  50.0 0.0 copy-start
  50.1 1.7 %collective-permute-done = f32[332,4,128]{2,1,0:T(4,128)S(1)} collective-permute-done((f32[332,4,128]{2,1,0:T(4,128)S(1)}, f32[332,4,128]{2,1,0:T(4,128)S(1)}, u32[]{:S(2)}, u32[]{:S(2)}) %collective-permute-start) | collective-permute-done | bytes 679968 | tf_op jit(solution)/shard_map/ppermute | solution.py:446
  51.8 0.0 copy-done.1
  51.8 0.0 copy-done
  51.8 11.7 %gather.1 = (f32[8,3,512]{2,1,0:T(4,128)S(1)}, f32[3,512]{1,0:T(4,128)S(1)}, f32[3,512]{1,0:T(4,128)S(1)}) custom-call(s32[1]{0:T(128)} %bitcast.where_ref, f32[1328,128]{1,0:T(8,128)S(1)} %bitcast.7, f32[1328,128]{1,0:T(8,128)S(1)} %bitcast.8, f32[3,512]{1,0:T(4,128)S(1)} %copy-done, f32[3,512]{1,0:T(4,128)S(1)} %copy-done.1), custom_call_target="tpu_custom_call" | custom-call | tf_op jit(solution)/shard_map/gather/pallas_call | solution.py:378
  63.5 9.3 %all_to_all.17 = f32[8,3,512]{2,1,0:T(4,128)S(1)} all-to-all(f32[8,3,512]{2,1,0:T(4,128)S(1)} %get-tuple-element.14), channel_id=1, replica_groups=mesh['grp'=4,'dev_0'=16,'dev_1'=4,'dev_2'=2] {'grp','dev_2'}, dimensions={0} | all-to-all | bytes 98304 | tf_op jit(solution)/shard_map/all_to_all | solution.py:459
  72.9 0.6 multiply_add_fusion
  (1 shorter events, 0.0 us)
Async XLA Ops:
  30.5 11.6 %copy-start.2 = (f32[12,4,128]{2,1,0:T(4,128)S(1)}, f32[12,4,128]{2,1,0:T(4,128)}, u32[]{:S(2)}) copy-start(f32[12,4,128]{2,1,0:T(4,128)} %get-tuple-element.11) | copy-start | bytes 73732
  42.3 9.5 %collective-permute-start = (f32[332,4,128]{2,1,0:T(4,128)S(1)}, f32[332,4,128]{2,1,0:T(4,128)S(1)}, u32[]{:S(2)}, u32[]{:S(2)}) collective-permute-start(f32[332,4,128]{2,1,0:T(4,128)S(1)} %pad_maximum_fusion), channel_id=1, source_target_pairs={{0,1},{1,0},{2,3},{3,2},{4,5},{5,4},{6,7},{7,6},{8,9},{9,8},{10,11... | collective-permute-start | bytes 2039816 | tf_op jit(solution)/shard_map/ppermute | solution.py:446
  50.0 1.7 %copy-start.1 = (f32[3,512]{1,0:T(4,128)S(1)}, f32[3,512]{1,0:T(4,128)}, u32[]{:S(2)}) copy-start(f32[3,512]{1,0:T(4,128)} %albedo_ref.1) | copy-start | bytes 18436
  50.0 1.7 %copy-start = (f32[3,512]{1,0:T(4,128)S(1)}, f32[3,512]{1,0:T(4,128)}, u32[]{:S(2)}) copy-start(f32[3,512]{1,0:T(4,128)} %emit_ref.1) | copy-start | bytes 18436

commit v7 on v5

--- a/solution.py
+++ b/solution.py
@@ -99,8 +99,7 @@
     rows += [ordered[0:1, :TILE], ordered[0:1, TILE:] + offsets]
     for piece in range(PACK // 4):
         part = jnp.concatenate(rows[piece * 4 : piece * 4 + 4], axis=0)
-        for peer in range(pack_out.shape[0]):
-            pack_out[peer, piece] = part
+        pack_out[piece] = part
     local = [row for field in nodes for row in lane_rows(field)]
     local += lane_rows(parent[...].astype(jnp.float32))
     local += [jnp.zeros((1, TILE), jnp.float32)] * (local_out.shape[0] * 4 - len(local))
@@ -423,7 +422,7 @@
     held, local = pl.pallas_call(
         pack_kernel,
         out_shape=(
-            jax.ShapeDtypeStruct((sizes[0], PACK // 4, 4, TILE), jnp.float32),
+            jax.ShapeDtypeStruct((PACK // 4, 4, TILE), jnp.float32),
             jax.ShapeDtypeStruct((own_rows // 4, 4, TILE), jnp.float32),
         ),
         in_specs=[vmem] * 8,
@@ -439,7 +438,9 @@
         block_source,
         block_count,
     )
-    held = lax.all_to_all(held, DEV[0], 0, 0, tiled=True).reshape(-1, 4, TILE)
+    held = lax.all_to_all(
+        jnp.broadcast_to(held[None], (sizes[0], *held.shape)), DEV[0], 0, 0, tiled=True
+    ).reshape(-1, 4, TILE)
     held = lax.all_to_all(
         jnp.broadcast_to(held[None], (sizes[1], *held.shape)), DEV[1], 0, 0, tiled=True
     )

time: 74.2 us -> 74.3 us (level)
  no operation moved by 1% of the time
where the time goes in v7:
time: 74.3 us; the launch traced here: 73.8 us
  blocking collectives  48.7 us (66%)
  Pallas kernels  13.3 us (18%)
  starting transfers between devices  7.71 us (10%)
  waiting for transfers between devices  1.71 us (2%)
  local copies, waits for them, and re-layouts  0.83 us (1%)
  other arithmetic  0.78 us (1%)
    all_to_all x1, blocking collectives, body(): lax.all_to_all(jnp.broadcast_to(held[None], (sizes[0], *held.shape)), DEV...  27.8 us
    all_to_all x1, blocking collectives, body(): lax.all_to_all(jnp.broadcast_to(held[None], (sizes[1], *held.shape)), DEV...  11.6 us
    pallas_call x1, Pallas kernels, gather_call(): pl.pallas_call(functools.partial(gather_kernel, sizes=sizes, node_count=n...  11.6 us
    all_to_all x1, blocking collectives, body(): lax.all_to_all(partial, ('grp', DEV[2]), 0, 0, tiled=True).sum(axis=0)  9.32 us
    ppermute x1, starting transfers between devices, body(): other = lax.ppermute(held, DEV[2], [(0, 1), (1, 0)])  7.71 us
    pallas_call x1, Pallas kernels, body(): pl.pallas_call(pack_kernel, out_shape=(jax.ShapeDtypeStruct((PACK // 4, 4...  1.76 us
    ppermute x1, waiting for transfers between devices, body(): other = lax.ppermute(held, DEV[2], [(0, 1), (1, 0)])  1.71 us
  transfers between devices with their start and end apart: 1, of which 1 were waited for; matrix products, arithmetic and copies ran while one was open for 0% of the time, Pallas kernels for 0%

profile of v7, /device:TPU:1, one launch (start us, length us, event | category | flops | bytes accessed | tf_op | source)
XLA Modules:
  0.0 73.8 jit_solution(18292191105085986357)
XLA Ops:
  0.7 1.8 %pack.1 = (f32[5,4,128]{2,1,0:T(4,128)}, f32[12,4,128]{2,1,0:T(4,128)}) custom-call(f32[3,512]{1,0:T(4,128)} %radiosity.1, f32[1,512]{1,0:T(1,128)} %bitcast.11, s32[1,512]{1,0:T(1,128)} %bitcast.12, f32[3,768]{1,0:T(4,128)} %position.1, f32[2,768]{1,0:T(2,128)} %angles.1, s32[1,128]{1,0:T(1,128)} %receiver.1, s32[1,128]{1,0:T(1,128)} %source.1, ...), custom_call_target="tpu_custom_call" | custom-call | tf_op jit(solution)/shard_map/pack/pallas_call | solution.py:422
  2.4 0.7 broadcast_in_dim.21
  3.1 27.8 %all_to_all.15 = f32[16,5,4,128]{3,2,1,0:T(4,128)S(1)} all-to-all(f32[16,5,4,128]{3,2,1,0:T(4,128)S(1)} %broadcast_in_dim.21), channel_id=1, replica_groups=mesh['grp'=4,'dev_0'=16,'dev_1'=4,'dev_2'=2] {'dev_0'}, dimensions={0} | all-to-all | bytes 327680 | tf_op jit(solution)/shard_map/all_to_all | solution.py:441
  30.9 0.1 broadcast_in_dim.23
  31.0 0.0 copy-start.2
  31.0 11.6 %all_to_all.16 = f32[4,80,4,128]{3,2,1,0:T(4,128)S(1)} all-to-all(f32[4,80,4,128]{3,2,1,0:T(4,128)S(1)} %broadcast_in_dim.23), channel_id=1, replica_groups=mesh['grp'=4,'dev_0'=16,'dev_1'=4,'dev_2'=2] {'dev_1'}, dimensions={0} | all-to-all | bytes 1310720 | tf_op jit(solution)/shard_map/all_to_all | solution.py:444
  42.6 0.0 copy-done.2
  42.6 0.1 pad_maximum_fusion
  42.8 7.7 %collective-permute-start = (f32[332,4,128]{2,1,0:T(4,128)S(1)}, f32[332,4,128]{2,1,0:T(4,128)S(1)}, u32[]{:S(2)}, u32[]{:S(2)}) collective-permute-start(f32[332,4,128]{2,1,0:T(4,128)S(1)} %pad_maximum_fusion), channel_id=1, source_target_pairs={{0,1},{1,0},{2,3},{3,2},{4,5},{5,4},{6,7},{7,6},{8,9},{9,8},{10,11... | collective-permute-start | bytes 2039816 | tf_op jit(solution)/shard_map/ppermute | solution.py:448
  50.5 0.0 copy-start.1
  50.5 0.0 copy-start
  50.5 1.7 %collective-permute-done = f32[332,4,128]{2,1,0:T(4,128)S(1)} collective-permute-done((f32[332,4,128]{2,1,0:T(4,128)S(1)}, f32[332,4,128]{2,1,0:T(4,128)S(1)}, u32[]{:S(2)}, u32[]{:S(2)}) %collective-permute-start) | collective-permute-done | bytes 679968 | tf_op jit(solution)/shard_map/ppermute | solution.py:448
  52.2 0.0 copy-done.1
  52.2 0.0 copy-done
  52.2 11.6 %gather.1 = (f32[8,3,512]{2,1,0:T(4,128)S(1)}, f32[3,512]{1,0:T(4,128)S(1)}, f32[3,512]{1,0:T(4,128)S(1)}) custom-call(s32[1]{0:T(128)} %bitcast.where_ref, f32[1328,128]{1,0:T(8,128)S(1)} %bitcast.7, f32[1328,128]{1,0:T(8,128)S(1)} %bitcast.8, f32[3,512]{1,0:T(4,128)S(1)} %copy-done, f32[3,512]{1,0:T(4,128)S(1)} %copy-done.1), custom_call_target="tpu_custom_call" | custom-call | tf_op jit(solution)/shard_map/gather/pallas_call | solution.py:378
  63.8 9.3 %all_to_all.17 = f32[8,3,512]{2,1,0:T(4,128)S(1)} all-to-all(f32[8,3,512]{2,1,0:T(4,128)S(1)} %get-tuple-element.14), channel_id=1, replica_groups=mesh['grp'=4,'dev_0'=16,'dev_1'=4,'dev_2'=2] {'grp','dev_2'}, dimensions={0} | all-to-all | bytes 98304 | tf_op jit(solution)/shard_map/all_to_all | solution.py:461
  73.2 0.6 multiply_add_fusion
  (1 shorter events, 0.0 us)
Async XLA Ops:
  31.0 11.6 %copy-start.2 = (f32[12,4,128]{2,1,0:T(4,128)S(1)}, f32[12,4,128]{2,1,0:T(4,128)}, u32[]{:S(2)}) copy-start(f32[12,4,128]{2,1,0:T(4,128)} %get-tuple-element.11) | copy-start | bytes 73732
  42.8 9.5 %collective-permute-start = (f32[332,4,128]{2,1,0:T(4,128)S(1)}, f32[332,4,128]{2,1,0:T(4,128)S(1)}, u32[]{:S(2)}, u32[]{:S(2)}) collective-permute-start(f32[332,4,128]{2,1,0:T(4,128)S(1)} %pad_maximum_fusion), channel_id=1, source_target_pairs={{0,1},{1,0},{2,3},{3,2},{4,5},{5,4},{6,7},{7,6},{8,9},{9,8},{10,11... | collective-permute-start | bytes 2039816 | tf_op jit(solution)/shard_map/ppermute | solution.py:448
  50.5 1.7 %copy-start.1 = (f32[3,512]{1,0:T(4,128)S(1)}, f32[3,512]{1,0:T(4,128)}, u32[]{:S(2)}) copy-start(f32[3,512]{1,0:T(4,128)} %albedo_ref.1) | copy-start | bytes 18436
  50.5 1.7 %copy-start = (f32[3,512]{1,0:T(4,128)S(1)}, f32[3,512]{1,0:T(4,128)}, u32[]{:S(2)}) copy-start(f32[3,512]{1,0:T(4,128)} %emit_ref.1) | copy-start | bytes 18436
